TPU v7x, 256 devices: a whole 4x4x8 slice. The times are simulated.
256 devices in a mesh: seq: 64 (over y, z, core), head: 4 (over x).
Axes of the slice: x: 4, y: 4, z: 8, core: 2. Of those that a mesh axis runs over, the one named last changes fastest.
Arguments:
- queries: bfloat16 [12288, 4096], P('seq', 'head'), may hold values from -125 to 125
- key_vectors: bfloat16 [12288, 4096], P('seq', 'head'), may hold values from -21 to 21
- values: bfloat16 [12288, 4096], P('seq', 'head'), may hold values from -6 to 6
- cotangent: bfloat16 [12288, 4096], P('seq', 'head'), may hold values from -6 to 6
- cluster: int32 [12288, 1], P('seq'), may hold values from 0 to 15; in each aligned block of 192 rows (0 to 191, 192 to 383, ...) at most 24 rows name the same one
- block_pattern: int32 [16, 96, 96], replicated, may hold values from 0 to 1, as said below
Outputs:
- attended: bfloat16 [12288, 4096], P('seq', 'head')
- query_grad: bfloat16 [12288, 4096], P('seq', 'head')
- key_grad: bfloat16 [12288, 4096], P('seq', 'head')
- value_grad: bfloat16 [12288, 4096], P('seq', 'head')
Inputs may be any that keep to these rules, and one draw needn't show every extreme that they name: Within the rows of one device no cluster is named by more than 24 rows, and in every draw some cluster is named by exactly 24 rows of some device. Every diagonal entry block_pattern[g, b, b] is 1.
All inputs are finite; a program needn't handle non-finite values.
Results may differ from a plain program's by a relative error of at most 0.0061.
Values may be sent and summed in bfloat16 or wider, within the bound.
A program may use at most 128 MiB of HBM per device.

v0:
```python
import jax
import jax.numpy as jnp
from jax import lax
from jax.sharding import PartitionSpec as P

HEADS = 32
HEAD_DIM = 128
GS = 4
BLK = 128


NEG_FILL = -1e30
EPSILON = 1e-05


def from_partner(value, axis, bit):
    mask = 2**bit
    pairs = [(source, source ^ mask) for source in range(lax.axis_size(axis))]
    return lax.ppermute(value, axis, pairs)


def contract_last(left_side, right_side):
    return lax.dot_general(
        left_side, right_side, (((1,), (1,)), ((), ())), preferred_element_type=jnp.float32
    )


def contract_first(left_side, right_side):
    return lax.dot_general(
        left_side, right_side, (((0,), (0,)), ((), ())), preferred_element_type=jnp.float32
    )


def visible_mask(pattern, query_pos, query_live, key_pos, key_live):
    pattern_rows = pattern[query_pos // BLK]
    allowed = jnp.take(pattern_rows, key_pos // BLK, axis=1) == 1
    causal = key_pos[None, :] <= query_pos[:, None]
    return allowed & causal & query_live[:, None] & key_live[None, :]


def cluster_ranks(table, cluster_index):
    source_count, tok_count = table.shape
    in_cluster = table == cluster_index
    token_iota = jnp.arange(tok_count, dtype=jnp.int32)
    earlier_table = (token_iota[:, None] < token_iota[None, :]).astype(jnp.bfloat16)
    earlier = jnp.dot(
        in_cluster.astype(jnp.bfloat16), earlier_table, preferred_element_type=jnp.float32
    ).astype(jnp.int32)
    global_pos = (
        jnp.arange(source_count, dtype=jnp.int32)[:, None] * tok_count + token_iota[None, :]
    )
    return (in_cluster, earlier, global_pos)


def code_positions(slot_code, global_pos, capacity):
    matches = slot_code[:, :, None] == jnp.arange(capacity, dtype=jnp.int32)[None, None, :]
    positions = jnp.sum(jnp.where(matches, global_pos[:, :, None], 0), axis=1)
    occupied = jnp.any(matches, axis=1)
    return (positions, occupied)


def slot_positions(table, cluster_index, slot_count):
    source_count = table.shape[0]
    capacity = GS * slot_count
    in_cluster, earlier, global_pos = cluster_ranks(table, cluster_index)
    slot_code = jnp.where(in_cluster, earlier % GS * slot_count + earlier // GS, -1)
    positions, occupied = code_positions(slot_code, global_pos, capacity)
    positions = (
        positions.reshape(source_count, GS, slot_count)
        .transpose(1, 0, 2)
        .reshape(GS, source_count * slot_count)
    )
    occupied = (
        occupied.reshape(source_count, GS, slot_count)
        .transpose(1, 0, 2)
        .reshape(GS, source_count * slot_count)
    )
    return (positions, occupied)


def swap_keys(piece_now, bit_index):
    return from_partner(piece_now, "seq", bit_index)


def swap_grads(piece_now, bit_index):
    return from_partner(piece_now, "seq", bit_index)


def dispatch_rows(outgoing):
    return lax.all_to_all(outgoing, "seq", split_axis=1, concat_axis=1, tiled=True)


def combine_rows(outgoing):
    return lax.all_to_all(outgoing, "seq", split_axis=1, concat_axis=1, tiled=True)


def collect(local_piece, member, along, swapper):
    combined = local_piece
    for bit_index in range(GS.bit_length() - 1):
        partner_piece = swapper(combined, bit_index)
        lower_side = member // 2**bit_index % 2 == 0
        combined = jnp.where(
            lower_side,
            jnp.concatenate([combined, partner_piece], along),
            jnp.concatenate([partner_piece, combined], along),
        )
    return combined


def reduce_to_member(all_terms, member, swapper):
    current = all_terms
    for bit_index in reversed(range(GS.bit_length() - 1)):
        half_rows = current.shape[1] // 2
        lower_side = member // 2**bit_index % 2 == 0
        low_half = current[:, :half_rows]
        high_half = current[:, half_rows:]
        kept = jnp.where(lower_side, low_half, high_half)
        given = jnp.where(lower_side, high_half, low_half)
        current = kept + swapper(given, bit_index)
    return current


def forward_heads(query_slots, key_slots, value_slots, grad_slots, visible, score_scale):
    query_count, features = query_slots.shape
    key_count = key_slots.shape[0]
    head_count = features // HEAD_DIM
    attended = jnp.zeros((query_count, features), jnp.bfloat16)
    query_grad = jnp.zeros((query_count, features), jnp.bfloat16)
    side_result = jnp.zeros((2, key_count, features), jnp.float32)

    def one_head(head_index, running):
        attended_acc, query_acc, side_acc = running
        column_start = head_index * HEAD_DIM
        query_rows = lax.dynamic_slice_in_dim(query_slots, column_start, HEAD_DIM, 1)
        key_rows = lax.dynamic_slice_in_dim(key_slots, column_start, HEAD_DIM, 1)
        value_rows = lax.dynamic_slice_in_dim(value_slots, column_start, HEAD_DIM, 1)
        grad_rows = lax.dynamic_slice_in_dim(grad_slots, column_start, HEAD_DIM, 1)
        scores = jnp.where(visible, contract_last(query_rows, key_rows) * score_scale, NEG_FILL)
        row_max = jnp.max(scores, axis=1, keepdims=True)
        weights = jnp.where(visible, jnp.exp(scores - row_max), 0.0)
        row_total = jnp.maximum(jnp.sum(weights, axis=1, keepdims=True), 1.0)
        probabilities = weights / row_total
        prob_half = probabilities.astype(jnp.bfloat16)
        attended_head = jnp.dot(prob_half, value_rows, preferred_element_type=jnp.float32).astype(
            jnp.bfloat16
        )
        prob_grad = contract_last(grad_rows, value_rows)
        row_delta = jnp.sum(probabilities * prob_grad, axis=1, keepdims=True)
        score_grad = (probabilities * (prob_grad - row_delta)).astype(jnp.bfloat16)
        query_head = (
            jnp.dot(score_grad, key_rows, preferred_element_type=jnp.float32) * score_scale
        ).astype(jnp.bfloat16)
        attended_acc = lax.dynamic_update_slice_in_dim(attended_acc, attended_head, column_start, 1)
        query_acc = lax.dynamic_update_slice_in_dim(query_acc, query_head, column_start, 1)
        key_part = contract_first(score_grad, query_rows)
        value_part = contract_first(prob_half, grad_rows)
        side_acc = lax.dynamic_update_slice_in_dim(
            side_acc, jnp.stack([key_part, value_part]), column_start, 2
        )
        return (attended_acc, query_acc, side_acc)

    return lax.fori_loop(0, head_count, one_head, (attended, query_grad, side_result))


def per_device(queries, key_vectors, values, cotangent, cluster, block_pattern):
    seq_count = lax.axis_size("seq")
    tok_count, features = queries.shape
    slot_count = 2 * tok_count // seq_count
    received = seq_count * slot_count
    group_count = seq_count // GS
    score_scale = HEAD_DIM ** (-0.5)
    my_index = lax.axis_index("seq")
    group_index = my_index // GS
    member = my_index % GS
    key_float = key_vectors.astype(jnp.float32)
    square_sum = lax.psum(jnp.sum(key_float * key_float, axis=1), "head")
    key_rms = jnp.sqrt(square_sum / (HEADS * HEAD_DIM) + EPSILON)[:, None]
    normed_float = key_float / key_rms
    normed = normed_float.astype(jnp.bfloat16)
    own_ids = cluster[:, 0]
    everyone = lax.all_gather(own_ids, "seq", axis=0, tiled=True)
    table = everyone.reshape(seq_count, tok_count)
    token_iota = jnp.arange(tok_count, dtype=jnp.int32)
    onehot_own = (own_ids[:, None] == jnp.arange(group_count, dtype=jnp.int32)[None, :]).astype(
        jnp.bfloat16
    )
    before_table = (token_iota[:, None] > token_iota[None, :]).astype(jnp.bfloat16)
    before = jnp.dot(before_table, onehot_own, preferred_element_type=jnp.float32)
    own_rank = jnp.sum(before * onehot_own.astype(jnp.float32), axis=1).astype(jnp.int32)
    pattern = lax.dynamic_index_in_dim(block_pattern, group_index, 0, keepdims=False)
    stacked_inputs = jnp.stack([queries, normed, values, cotangent])
    destination = own_ids * GS + own_rank % GS
    send_slot = destination * slot_count + own_rank // GS
    outgoing = jnp.zeros((4, received, features), jnp.bfloat16).at[:, send_slot].set(stacked_inputs)
    arrived = dispatch_rows(outgoing)
    key_positions, key_present = slot_positions(table, group_index, slot_count)
    query_positions = lax.dynamic_index_in_dim(key_positions, member, 0, keepdims=False)
    query_present = lax.dynamic_index_in_dim(key_present, member, 0, keepdims=False)
    flat_positions = key_positions.reshape(-1)
    flat_present = key_present.reshape(-1)
    visible = visible_mask(pattern, query_positions, query_present, flat_positions, flat_present)
    key_value = collect(arrived[1:3], member, 1, swap_keys)
    attended, query_grad, both_terms = forward_heads(
        arrived[0], key_value[0], key_value[1], arrived[3], visible, score_scale
    )
    reduced = reduce_to_member(both_terms, member, swap_grads)
    key_part = reduced[0]
    value_part = reduced[1]
    normed_grad = (key_part * score_scale).astype(jnp.bfloat16)
    value_slots = value_part.astype(jnp.bfloat16)
    outgoing_back = jnp.stack([attended, query_grad, normed_grad, value_slots])
    returned = combine_rows(outgoing_back)
    home_rows = returned[:, send_slot]
    grad_float = home_rows[2].astype(jnp.float32)
    inner = lax.psum(jnp.sum(normed_float * grad_float, axis=1), "head")
    key_grad = (
        (grad_float - normed_float * (inner / (HEADS * HEAD_DIM))[:, None]) / key_rms
    ).astype(jnp.bfloat16)
    return (home_rows[0], home_rows[1], key_grad, home_rows[3])


def solution(mesh):
    in_specs = (
        P("seq", "head"),
        P("seq", "head"),
        P("seq", "head"),
        P("seq", "head"),
        P("seq", None),
        P(),
    )
    out_specs = (P("seq", "head"), P("seq", "head"), P("seq", "head"), P("seq", "head"))
    return jax.shard_map(
        per_device, mesh=mesh, in_specs=in_specs, out_specs=out_specs, check_vma=False
    )
```

profile of v0, /device:TPU:1, one launch (start us, length us, event | category | flops | bytes accessed | tf_op | source)
XLA Modules:
  0.0 935.7 jit_solution(13777769954462944271)
XLA Ops:
  3.5 9.3 psum.14
  19.0 22.8 %scatter_fusion = bf16[4,384,1024]{2,0,1:T(4,128)(2,1)} fusion(bf16[4,384,1024]{2,0,1:T(4,128)(2,1)} %broadcast_in_dim.72, s32[192]{0:T(256)S(1)} %bitcast.92, bf16[192,4,1024]{2,1,0:T(4,128)(2,1)S(1)} %copy.35), kind=kCustom, calls=%fused_computation.3 | custom fusion | bytes 4719360 | tf_op jit(solution)/shard_map/scatter | solution.py:194
  41.8 87.8 %all_to_all.10 = bf16[4,384,1024]{2,0,1:T(4,128)(2,1)S(1)} all-to-all(bf16[4,384,1024]{2,0,1:T(4,128)(2,1)} %scatter_fusion), channel_id=1, replica_groups=mesh['seq'=64,'head'=4] {'seq'}, dimensions={1} | all-to-all | bytes 6291456 | tf_op jit(solution)/shard_map/all_to_all | solution.py:90
  134.8 243.3 %all-reduce = s32[12288]{0:T(1024)S(1)} all-reduce(s32[12288]{0:T(1024)S(1)} %dynamic-update-slice), channel_id=2, replica_groups=mesh['seq'=64,'head'=4] {'seq'}, use_global_device_ids=true, to_apply=%add | all-reduce | flops 12288 | bytes 98304
  378.1 16.6 %broadcast_select_fusion.2 = bf16[2,768,1024]{2,0,1:T(2,128)(2,1)} fusion(pred[]{:T(512)S(6)} %eq.66, bf16[2,384,1024]{2,0,1:T(2,128)(2,1)} %collective-permute-done, bf16[2,384,1024]{2,0,1:T(2,128)(2,1)S(1)} %slice.68), kind=kLoop, calls=%fused_computation.41 | loop fusion | flops 4718592 | bytes 6291457 | tf_op jit(solution)/shard_map/jit(_where)/select_n | solution.py:102
  410.2 49.1 %collective-permute-done.1 = bf16[2,768,1024]{2,0,1:T(2,128)(2,1)} collective-permute-done((bf16[2,768,1024]{2,0,1:T(2,128)(2,1)}, bf16[2,768,1024]{2,0,1:T(2,128)(2,1)}, u32[]{:S(2)}, u32[]{:S(2)}) %collective-permute-start.1) | collective-permute-done | bytes 3145760 | tf_op jit(solution)/shard_map/ppermute | solution.py:19
  459.2 30.7 %broadcast_select_fusion = bf16[2,1536,1024]{2,0,1:T(2,128)(2,1)S(1)} fusion(pred[]{:T(512)S(6)} %eq.65, bf16[2,768,1024]{2,0,1:T(2,128)(2,1)} %collective-permute-done.1, bf16[2,768,1024]{2,0,1:T(2,128)(2,1)} %broadcast_select_fusion.2), kind=kLoop, calls=%fused_computation.38 | loop fusion | flops 9437184 | bytes 12582913 | tf_op jit(solution)/shard_map/jit(_where)/select_n | solution.py:102
  490.0 9.8 %fusion.51 = (bf16[1,1536,1024]{2,0,1:T(2,128)(2,1)S(1)}, bf16[1,1536,1024]{2,0,1:T(2,128)(2,1)}) fusion(bf16[2,1536,1024]{2,0,1:T(2,128)(2,1)S(1)} %broadcast_select_fusion), kind=kLoop, calls=%fused_computation.137 | loop fusion | bytes 12582912 | tf_op jit(solution)/shard_map/slice | solution.py:204
  499.8 8.0 copy_bitcast_fusion
  512.8 143.0 %while.17 = (s32[]{:T(128)}, bf16[384,1024]{1,0:T(8,128)(2,1)S(1)}, bf16[384,1024]{1,0:T(8,128)(2,1)S(1)}, f32[2,1536,1024]{2,0,1:T(2,128)}, bf16[384,1024]{1,0:...) while((s32[]{:T(128)}, bf16[384,1024]{1,0:T(8,128)(2,1)S(1)}, ...), condition=%wide.region_10.11_spmd, body=%wide.region_6.10_spmd.sunk | while | flops 915946752 | bytes 36587200 | solution.py:162
  534.1 6.7 copy_dynamic-update-slice_fusion.2
  550.5 6.7 copy_dynamic-update-slice_fusion.2
  567.0 6.7 copy_dynamic-update-slice_fusion.2
  583.4 6.7 copy_dynamic-update-slice_fusion.2
  616.3 6.7 copy_dynamic-update-slice_fusion.2
  632.7 6.7 copy_dynamic-update-slice_fusion.2
  649.2 6.7 copy_dynamic-update-slice_fusion.2
  655.8 10.5 %broadcast_select_fusion.1 = f32[2,768,1024]{2,0,1:T(2,128)} fusion(pred[]{:T(512)S(6)} %eq.65, f32[2,1536,1024]{2,0,1:T(2,128)} %get-tuple-element.162), kind=kLoop, calls=%fused_computation.40 | loop fusion | flops 1572864 | bytes 18874368 | tf_op jit(solution)/shard_map/jit(_where)/select_n | solution.py:118
  666.6 130.5 %collective-permute-done.2 = f32[2,768,1024]{2,0,1:T(2,128)S(1)} collective-permute-done((f32[2,768,1024]{2,0,1:T(2,128)}, f32[2,768,1024]{2,0,1:T(2,128)S(1)}, u32[]{:S(2)}, u32[]{:S(2)}) %collective-permute-start.2) | collective-permute-done | bytes 6291488 | tf_op jit(solution)/shard_map/ppermute | solution.py:19
  797.0 10.0 %select_add_fusion = f32[2,768,1024]{2,0,1:T(2,128)S(1)} fusion(f32[2,768,1024]{2,0,1:T(2,128)S(1)} %collective-permute-done.2, pred[]{:T(512)S(6)} %eq.65, f32[2,1536,1024]{2,0,1:T(2,128)} %get-tuple-element.162), kind=kLoop, calls=%fused_computation.39 | loop fusion | flops 3145728 | bytes 25165824 | tf_op jit(solution)/shard_map/add | solution.py:119
  808.7 7.5 collective-permute-start.3
  827.4 8.4 pad_maximum_fusion.1
  835.7 8.9 all-to-all-start.1
  844.7 73.4 %all-to-all-done.1 = bf16[4,384,1024]{2,0,1:T(4,128)(2,1)} async-done(((bf16[4,384,1024]{2,0,1:T(4,128)(2,1)}), bf16[4,384,1024]{2,0,1:T(4,128)(2,1)}, u32[]{:S(2)}, u32[]{:S(2)}) %all-to-all-start.1) | async-done | bytes 3145760 | tf_op jit(solution)/shard_map/all_to_all | solution.py:94
  (167 shorter events, 148.4 us)
Async XLA Ops:
  0.6 398.4 %copy-start = (s32[16,96,96]{2,1,0:T(8,128)S(1)}, s32[16,96,96]{2,1,0:T(8,128)}, u32[]{:S(2)}) copy-start(s32[16,96,96]{2,1,0:T(8,128)} %param.13) | copy-start | bytes 1769476
  129.6 1.7 copy-start.2
  131.3 1.9 copy-start.7
  131.3 3.2 copy-start.6
  133.1 245.0 %collective-permute-start = (bf16[2,384,1024]{2,0,1:T(2,128)(2,1)S(1)}, bf16[2,384,1024]{2,0,1:T(2,128)(2,1)}, u32[]{:S(2)}, u32[]{:S(2)}) collective-permute-start(bf16[2,384,1024]{2,0,1:T(2,128)(2,1)S(1)} %slice.68), channel_id=1, source_target_pairs={{0,4},{4,0},{8,12},{12,8},{16,20},{20,16},{24,28},{28,24},{32,36},... | collective-permute-start | bytes 4718600 | tf_op jit(solution)/shard_map/ppermute | solution.py:19
  394.7 64.6 %collective-permute-start.1 = (bf16[2,768,1024]{2,0,1:T(2,128)(2,1)}, bf16[2,768,1024]{2,0,1:T(2,128)(2,1)}, u32[]{:S(2)}, u32[]{:S(2)}) collective-permute-start(bf16[2,768,1024]{2,0,1:T(2,128)(2,1)} %broadcast_select_fusion.2), channel_id=1, source_target_pairs={{0,8},{4,12},{8,0},{12,4},{16,24},{20,28},{24,16},{28,20},{32,40},... | collective-permute-start | bytes 9437192 | tf_op jit(solution)/shard_map/ppermute | solution.py:19
  404.1 2.3 copy-start.3
  666.3 130.8 %collective-permute-start.2 = (f32[2,768,1024]{2,0,1:T(2,128)}, f32[2,768,1024]{2,0,1:T(2,128)S(1)}, u32[]{:S(2)}, u32[]{:S(2)}) collective-permute-start(f32[2,768,1024]{2,0,1:T(2,128)} %broadcast_select_fusion.1), channel_id=1, source_target_pairs={{0,8},{4,12},{8,0},{12,4},{16,24},{20,28},{24,16},{28,20},{32,40},... | collective-permute-start | bytes 18874376 | tf_op jit(solution)/shard_map/ppermute | solution.py:19
  808.7 12.7 %collective-permute-start.3 = (f32[2,384,1024]{2,0,1:T(2,128)S(1)}, f32[2,384,1024]{2,0,1:T(2,128)S(1)}, u32[]{:S(2)}, u32[]{:S(2)}) collective-permute-start(f32[2,384,1024]{2,0,1:T(2,128)S(1)} %broadcast_select_fusion.3), channel_id=1, source_target_pairs={{0,4},{4,0},{8,12},{12,8},{16,20},{20,16},{24,28},{28,24},{32,36},... | collective-permute-start | bytes 9437192 | tf_op jit(solution)/shard_map/ppermute | solution.py:19
  835.7 82.3 %all-to-all-start.1 = ((bf16[4,384,1024]{2,0,1:T(4,128)(2,1)}), bf16[4,384,1024]{2,0,1:T(4,128)(2,1)}, u32[]{:S(2)}, u32[]{:S(2)}) async-start(bf16[4,384,1024]{2,0,1:T(4,128)(2,1)} %pad_maximum_fusion.1), calls=%async_computation.1 | async-start | bytes 6291456 | tf_op jit(solution)/shard_map/all_to_all | solution.py:94
  924.9 1.7 copy-start.4
  924.9 9.5 %copy-start.5 = (bf16[1,192,1024]{2,0,1:T(2,128)(2,1)S(1)}, bf16[1,192,1024]{2,0,1:T(2,128)(2,1)}, u32[]{:S(2)}) copy-start(bf16[1,192,1024]{2,0,1:T(2,128)(2,1)} %get-tuple-element.226) | copy-start | bytes 1179652
  925.8 9.5 %copy-start.1 = (s32[16,96,96]{2,1,0:T(8,128)S(1)}, s32[16,96,96]{2,1,0:T(8,128)}, u32[]{:S(2)}) copy-start(s32[16,96,96]{2,1,0:T(8,128)} %param.13) | copy-start | bytes 1769476
where the time goes:
time: 946 us; the launch traced here: 936 us
  blocking collectives  347 us (37%)
  waiting for transfers between devices  256 us (27%)
  local copies, waits for them, and re-layouts  128 us (14%)
  other arithmetic  104 us (11%)
  matrix products  70.2 us (7%)
  starting transfers between devices  17 us (2%)
  loops' own time  11.8 us (1%)
    unnamed x1, blocking collectives  243 us
    ppermute x4, waiting for transfers between devices, from_partner(): return lax.ppermute(value, axis, pairs)  182 us
    all_to_all x1, blocking collectives, dispatch_rows(): lax.all_to_all(outgoing, 'seq', split_axis=1, concat_axis=1, tiled=True)  87.8 us
    all_to_all x1, waiting for transfers between devices, combine_rows(): lax.all_to_all(outgoing, 'seq', split_axis=1, concat_axis=1, tiled=True)  73.4 us
    dynamic_update_slice x8, local copies, waits for them, and re-layouts, one_head(): lax.dynamic_update_slice_in_dim(side_acc, jnp.stack([key_part, value_part...  53.5 us
    select_n x2, other arithmetic, collect(): jnp.where(lower_side, jnp.concatenate([combined, partner_piece], along),...  47.3 us
    dot_general x16, matrix products, contract_last(): lax.dot_general(left_side, right_side, (((1,), (1,)), ((), ())), preferre...  29.4 us
    scatter x1, local copies, waits for them, and re-layouts, per_device(): jnp.zeros((4, received, features), jnp.bfloat16).at[:, send_slot]  22.8 us
  transfers between devices with their start and end apart: 5, of which 4 were waited for; matrix products, arithmetic and copies ran while one was open for 2% of the time, Pallas kernels for 0%

commit v1 on v0

v1 whole, which is shorter than its diff:
```python
import functools

import jax
import jax.numpy as jnp
import numpy as np
from jax import lax
from jax.experimental import pallas as pl
from jax.experimental.pallas import tpu as pltpu
from jax.sharding import PartitionSpec as P

HEADS = 32
HEAD_DIM = 128
BLK = 128
EPSILON = 1e-05
CAP = 24
NZ = 8
ND = 8
T_DEV = 192
GROUPS = 16
PAIR = 2 * CAP
ROWS = GROUPS * PAIR
SLOTS = 64 * CAP
QB = SLOTS // 4
CH = 128
BIG = 1e30
MESH = pl.DeviceIdType.MESH
F32 = jnp.float32
BF16 = jnp.bfloat16


def contract_last(left_side, right_side):
    return lax.dot_general(
        left_side, right_side, (((1,), (1,)), ((), ())), preferred_element_type=F32
    )


def place():
    me = lax.axis_index("seq")
    core = lax.rem(me, 2)
    z = lax.rem(me // 2, NZ)
    y = me // (2 * NZ)
    return y, z, core


def along_z(y, core, z):
    return (y * NZ + z) * 2 + core


def along_d(d, z):
    return ((d // 2) * NZ + z) * 2 + lax.rem(d, 2)


def greet(y, z, core, d):
    barrier = pltpu.get_barrier_semaphore()

    def signal(k, carry):
        pl.semaphore_signal(
            barrier,
            inc=1,
            device_id={"seq": along_z(y, core, lax.rem(z + k, NZ))},
            device_id_type=MESH,
        )
        pl.semaphore_signal(
            barrier,
            inc=1,
            device_id={"seq": along_d(lax.rem(d + k, ND), z)},
            device_id_type=MESH,
        )
        return carry

    lax.fori_loop(1, 8, signal, 0)
    pl.semaphore_wait(barrier, 14)


def head_columns(z):
    return pl.ds(pl.multiple_of(z * HEAD_DIM, HEAD_DIM), HEAD_DIM)


def pair_columns(d):
    return pl.ds(pl.multiple_of(d * 128, 128), 128)


def expander(slot_row, second):
    rows = lax.broadcasted_iota(jnp.int32, (ROWS, T_DEV), 0)
    hit = rows == slot_row[:, :T_DEV] + CAP * second
    return jnp.where(hit, 1.0, 0.0).astype(BF16)


def dispatch_kernel(
    slot_ref,
    meta_ref,
    v_ref,
    g_ref,
    q_ref,
    k_ref,
    out_ref,
    meta_out,
    slots_out,
    slots,
    metas,
    held,
    placing,
    sending,
    small_send,
    small_recv,
    meta_send,
    meta_recv,
    z_send,
    z_recv,
    d_send,
    d_recv,
    slots_sem,
):
    y, z, core = place()
    d = y * 2 + core
    sources = (v_ref, g_ref, q_ref, k_ref)
    greet(y, z, core, d)

    def small_copy(kind, k):
        to = lax.rem(z + k, NZ)
        if kind == 0:
            src, dst = slot_ref, slots.at[z]
        else:
            src, dst = meta_ref, metas.at[z]
        return pltpu.make_async_remote_copy(
            src_ref=src,
            dst_ref=dst,
            send_sem=small_send.at[kind, to],
            recv_sem=small_recv.at[kind, z],
            device_id={"seq": along_z(y, core, to)},
            device_id_type=MESH,
        )

    def small_arrival(kind, k):
        came = lax.rem(z + k, NZ)
        if kind == 0:
            src, dst = slot_ref, slots.at[came]
        else:
            src, dst = meta_ref, metas.at[came]
        return pltpu.make_async_remote_copy(
            src_ref=src,
            dst_ref=dst,
            send_sem=small_send.at[kind, came],
            recv_sem=small_recv.at[kind, came],
            device_id={"seq": along_z(y, core, came)},
            device_id_type=MESH,
        )

    def z_copy(a, k):
        to = lax.rem(z + k, NZ)
        return pltpu.make_async_remote_copy(
            src_ref=sources[a].at[:, head_columns(to)],
            dst_ref=held.at[a, z],
            send_sem=z_send.at[a, to],
            recv_sem=z_recv.at[a, z],
            device_id={"seq": along_z(y, core, to)},
            device_id_type=MESH,
        )

    def z_arrival(a, k):
        came = lax.rem(z + k, NZ)
        return pltpu.make_async_remote_copy(
            src_ref=held.at[a, came],
            dst_ref=held.at[a, came],
            send_sem=z_send.at[a, came],
            recv_sem=z_recv.at[a, came],
            device_id={"seq": along_z(y, core, came)},
            device_id_type=MESH,
        )

    def z_own(a):
        return pltpu.make_async_copy(
            sources[a].at[:, head_columns(z)], held.at[a, z], z_recv.at[a, z]
        )

    def d_copy(a, k):
        to = lax.rem(d + k, ND)
        return pltpu.make_async_remote_copy(
            src_ref=sending.at[a, :, to],
            dst_ref=out_ref.at[a, d],
            send_sem=d_send.at[a, to],
            recv_sem=d_recv.at[a, d],
            device_id={"seq": along_d(to, z)},
            device_id_type=MESH,
        )

    def d_arrival(a, k):
        came = lax.rem(d + k, ND)
        return pltpu.make_async_remote_copy(
            src_ref=out_ref.at[a, came],
            dst_ref=out_ref.at[a, came],
            send_sem=d_send.at[a, came],
            recv_sem=d_recv.at[a, came],
            device_id={"seq": along_d(came, z)},
            device_id_type=MESH,
        )

    def d_own(a):
        return pltpu.make_async_copy(sending.at[a, :, d], out_ref.at[a, d], d_recv.at[a, d])

    def meta_copy(k):
        to = lax.rem(d + k, ND)
        return pltpu.make_async_remote_copy(
            src_ref=metas.at[:, :, pair_columns(to)],
            dst_ref=meta_out.at[d],
            send_sem=meta_send.at[to],
            recv_sem=meta_recv.at[d],
            device_id={"seq": along_d(to, z)},
            device_id_type=MESH,
        )

    def meta_arrival(k):
        came = lax.rem(d + k, ND)
        return pltpu.make_async_remote_copy(
            src_ref=meta_out.at[came],
            dst_ref=meta_out.at[came],
            send_sem=meta_send.at[came],
            recv_sem=meta_recv.at[came],
            device_id={"seq": along_d(came, z)},
            device_id_type=MESH,
        )

    def meta_own():
        return pltpu.make_async_copy(
            metas.at[:, :, pair_columns(d)], meta_out.at[d], meta_recv.at[d]
        )

    def each(first, body):
        def step(k, carry):
            body(k)
            return carry

        lax.fori_loop(first, 8, step, 0)

    def start_small(k):
        small_copy(0, k).start()
        small_copy(1, k).start()

    each(1, start_small)
    own_slot = pltpu.make_async_copy(slot_ref, slots.at[z], small_recv.at[0, z])
    own_meta = pltpu.make_async_copy(meta_ref, metas.at[z], small_recv.at[1, z])
    own_slot.start()
    own_meta.start()
    for a in range(4):
        z_own(a).start()
        each(1, lambda k, a=a: z_copy(a, k).start())
    own_slot.wait()
    own_meta.wait()

    def finish_small(k):
        small_arrival(0, k).wait_recv()
        small_arrival(1, k).wait_recv()

    each(1, finish_small)
    keep_slots = pltpu.make_async_copy(slots, slots_out, slots_sem)
    keep_slots.start()
    meta_own().start()
    each(1, lambda k: meta_copy(k).start())

    def build(zz, carry):
        placing[zz] = expander(slots[zz], lax.rem(zz, 2))
        return carry

    lax.fori_loop(0, NZ, build, 0)

    def expand(a, carry):
        pltpu.make_async_copy(held.at[a, z], held.at[a, z], z_recv.at[a, z]).wait()
        each(1, lambda k: z_arrival(a, k).wait_recv())

        def pair(p, inner):
            rows = jnp.dot(placing[2 * p], held[a, 2 * p], preferred_element_type=F32)
            rows += jnp.dot(placing[2 * p + 1], held[a, 2 * p + 1], preferred_element_type=F32)
            sending[a, p] = rows.astype(BF16).reshape(ND, 2, PAIR, HEAD_DIM)
            return inner

        lax.fori_loop(0, NZ // 2, pair, 0)
        each(1, lambda k: d_copy(a, k).start())
        d_own(a).start()
        return carry

    lax.fori_loop(0, 4, expand, 0)

    def finish(a, carry):
        pltpu.make_async_copy(out_ref.at[a, d], out_ref.at[a, d], d_recv.at[a, d]).wait()

        def one(k):
            d_arrival(a, k).wait_recv()
            d_arrival(a, k).wait_send()
            z_arrival(a, k).wait_send()

        each(1, one)
        return carry

    lax.fori_loop(0, 4, finish, 0)
    keep_slots.wait()
    meta_own().wait()

    def finish_meta(k):
        small_arrival(0, k).wait_send()
        small_arrival(1, k).wait_send()
        meta_arrival(k).wait_recv()
        meta_arrival(k).wait_send()

    each(1, finish_meta)


def dispatch(slot_row, meta_row, v, g, q, k):
    any_space = pl.BlockSpec(memory_space=pl.ANY)
    dma = pltpu.SemaphoreType.DMA
    return pl.pallas_call(
        dispatch_kernel,
        out_shape=(
            jax.ShapeDtypeStruct((4, ND, NZ // 2, 2, PAIR, HEAD_DIM), BF16),
            jax.ShapeDtypeStruct((ND, NZ, 1, 128), F32),
            jax.ShapeDtypeStruct((NZ, 1, 256), jnp.int32),
        ),
        in_specs=[any_space] * 6,
        out_specs=(any_space,) * 3,
        scratch_shapes=[
            pltpu.VMEM((NZ, 1, 256), jnp.int32),
            pltpu.VMEM((NZ, 1, 1024), F32),
            pltpu.VMEM((4, NZ, T_DEV, HEAD_DIM), BF16),
            pltpu.VMEM((NZ, ROWS, T_DEV), BF16),
            pltpu.VMEM((4, NZ // 2, ND, 2, PAIR, HEAD_DIM), BF16),
            dma((2, NZ)),
            dma((2, NZ)),
            dma((ND,)),
            dma((ND,)),
            dma((4, NZ)),
            dma((4, NZ)),
            dma((4, ND)),
            dma((4, ND)),
            dma,
        ],
        compiler_params=pltpu.CompilerParams(collective_id=0, has_side_effects=True),
        name="dispatch",
    )(slot_row, meta_row, v, g, q, k)


def attention_kernel(
    score_scale,
    meta_ref,
    rep_ref,
    pick_ref,
    base_ref,
    pattern_ref,
    order_ref,
    v_ref,
    g_ref,
    q_ref,
    k_ref,
    o_ref,
    dq_ref,
    dk_ref,
    dv_ref,
    keys,
    queries,
    values,
    grads,
    key_t,
    value_t,
    scores,
    prob_grads,
    probs,
    score_grads,
    key_acc,
    value_acc,
):
    flat = (SLOTS, HEAD_DIM)
    numbers = jnp.dot(rep_ref[...], meta_ref[...].astype(BF16), preferred_element_type=F32)
    numbers = (numbers * pick_ref[...].astype(F32)).astype(BF16)
    number = jnp.dot(numbers, jnp.ones((128, 128), BF16), preferred_element_type=F32)
    lane = lax.broadcasted_iota(jnp.int32, flat, 1).astype(F32)
    position = base_ref[...].astype(F32) * 64.0 + number - 1.0
    low = lane * float(BLK)
    here = (number > 0.5) & (position >= low) & (position < low + float(BLK))
    dead = (number < 0.5) & (lane == 96.0)
    block = jnp.where(here | dead, 1.0, 0.0).astype(BF16)
    keys[:, :HEAD_DIM] = k_ref[...].reshape(flat)
    keys[:, HEAD_DIM:] = block
    queries[:, :HEAD_DIM] = q_ref[...].reshape(flat)
    hidden = jnp.dot(block, pattern_ref[...], preferred_element_type=F32)
    queries[:, HEAD_DIM:] = hidden.astype(BF16)
    values[...] = v_ref[...].reshape(flat)
    grads[...] = g_ref[...].reshape(flat)
    across = lax.broadcasted_iota(jnp.int32, (QB, QB), 1)
    eye = jnp.where(lax.broadcasted_iota(jnp.int32, (QB, QB), 0) == across, 1.0, 0.0).astype(BF16)
    small_eye = eye[:HEAD_DIM, :HEAD_DIM]
    key_t[...] = contract_last(small_eye, keys[:, :HEAD_DIM]).astype(BF16)
    value_t[...] = contract_last(small_eye, values[...]).astype(BF16)
    turn = score_scale * 1.4426950408889634

    def chunk(j, start=0):
        return pl.ds(pl.multiple_of(start + j * CH, CH), CH)

    def fold(piece, op):
        return op(piece.reshape(CH // 8, 8, QB), axis=0)

    for i in (3, 2, 1, 0):
        span = QB * (i + 1)
        query_rows = queries[QB * i : span, :]
        grad_rows = grads[QB * i : span, :]

        def full_scores(j, running):
            piece = contract_last(keys[chunk(j), :], query_rows)
            scores[chunk(j), :] = piece
            return jnp.maximum(running, fold(piece, jnp.max))

        def edge_scores(j, running):
            piece = contract_last(keys[chunk(j, QB * i), :], query_rows)
            piece += order_ref[chunk(j), :].astype(F32)
            scores[chunk(j, QB * i), :] = piece
            return jnp.maximum(running, fold(piece, jnp.max))

        top = jnp.full((8, QB), -3e38, F32)
        if i:
            top = lax.fori_loop(0, 3 * i, full_scores, top)
        top = lax.fori_loop(0, 3, edge_scores, top)
        top = jnp.max(top, axis=0, keepdims=True)

        def weigh(j, running):
            total, delta = running
            weights = jnp.exp2((scores[chunk(j), :] - top) * turn)
            scores[chunk(j), :] = weights
            terms = contract_last(values[chunk(j), :], grad_rows)
            prob_grads[chunk(j), :] = terms
            return (total + fold(weights, jnp.sum), delta + fold(weights * terms, jnp.sum))

        zero = jnp.zeros((8, QB), F32)
        total, delta = lax.fori_loop(0, 3 * (i + 1), weigh, (zero, zero))
        inverse = 1.0 / jnp.maximum(jnp.sum(total, axis=0, keepdims=True), 1.0)
        delta = jnp.sum(delta, axis=0, keepdims=True) * inverse

        def settle(j, carry):
            shares = scores[chunk(j), :] * inverse
            half = shares.astype(BF16)
            probs[chunk(j), :] = half
            slopes = (shares * (prob_grads[chunk(j), :] - delta)).astype(BF16)
            score_grads[chunk(j), :] = slopes
            value_part = jnp.dot(half, grad_rows, preferred_element_type=F32)
            key_part = jnp.dot(slopes, query_rows[:, :HEAD_DIM], preferred_element_type=F32)
            if i == 3:
                value_acc[chunk(j), :] = value_part
                key_acc[chunk(j), :] = key_part
            else:
                value_acc[chunk(j), :] += value_part
                key_acc[chunk(j), :] += key_part
            return carry

        lax.fori_loop(0, 3 * (i + 1), settle, 0)
        shape = (2, NZ // 2, PAIR, HEAD_DIM)
        attended_t = jnp.dot(value_t[:, :span], probs[:span, :], preferred_element_type=F32)
        attended = contract_last(eye, attended_t.astype(BF16))
        o_ref[2 * i : 2 * i + 2] = attended.astype(BF16).reshape(shape)
        query_t = jnp.dot(key_t[:, :span], score_grads[:span, :], preferred_element_type=F32)
        query_grad = contract_last(eye, (query_t * score_scale).astype(BF16))
        dq_ref[2 * i : 2 * i + 2] = query_grad.astype(BF16).reshape(shape)

    whole = (ND, NZ // 2, PAIR, HEAD_DIM)
    dk_ref[...] = (key_acc[...] * score_scale).astype(BF16).reshape(whole)
    dv_ref[...] = value_acc[...].astype(BF16).reshape(whole)


def slot_tables():
    order = np.arange(SLOTS)
    rank = order % CAP
    z = order // CAP % NZ
    d = order // (CAP * NZ)
    source = (d // 2) * 16 + z * 2 + d % 2
    arrival = d * NZ + z
    rep = (arrival[:, None] == np.arange(64)[None, :]).astype(np.float32)
    lanes = np.arange(128)[None, :]
    pick = np.stack([(lanes == (rank + CAP * unit)[:, None]) for unit in range(2)])
    base = np.broadcast_to((source * 3)[:, None], (SLOTS, 128)).astype(np.float32)
    sequence = (source * CAP + rank)[:QB]
    hidden = np.where(sequence[:, None] > sequence[None, :], -BIG, 0.0).astype(np.float32)
    return rep, pick.astype(np.float32), base, hidden


def attention(meta, pattern, arrived):
    rep, pick, base, hidden = slot_tables()
    fixed = lambda *zeros: lambda unit: zeros
    piece = (None, ND, NZ // 2, None, PAIR, HEAD_DIM)
    in_specs = [
        pl.BlockSpec((64, 128), fixed(0, 0)),
        pl.BlockSpec((SLOTS, 64), fixed(0, 0)),
        pl.BlockSpec((None, SLOTS, 128), lambda unit: (unit, 0, 0)),
        pl.BlockSpec((SLOTS, 128), fixed(0, 0)),
        pl.BlockSpec((None, 128, 128), lambda unit: (unit, 0, 0)),
        pl.BlockSpec((QB, QB), fixed(0, 0)),
    ]
    for a in range(4):
        in_specs.append(pl.BlockSpec(piece, lambda unit, a=a: (a, 0, 0, unit, 0, 0)))
    out_shape = jax.ShapeDtypeStruct((ND, NZ // 2, 2, PAIR, HEAD_DIM), BF16)
    out_spec = pl.BlockSpec(piece[1:], lambda unit: (0, 0, unit, 0, 0))
    vmem = pltpu.VMEM
    return pl.pallas_call(
        functools.partial(attention_kernel, HEAD_DIM ** (-0.5)),
        out_shape=(out_shape,) * 4,
        grid=(2,),
        in_specs=in_specs,
        out_specs=(out_spec,) * 4,
        scratch_shapes=[
            vmem((SLOTS, 256), BF16),
            vmem((SLOTS, 256), BF16),
            vmem((SLOTS, HEAD_DIM), BF16),
            vmem((SLOTS, HEAD_DIM), BF16),
            vmem((HEAD_DIM, SLOTS), BF16),
            vmem((HEAD_DIM, SLOTS), BF16),
            vmem((SLOTS, QB), F32),
            vmem((SLOTS, QB), F32),
            vmem((SLOTS, QB), BF16),
            vmem((SLOTS, QB), BF16),
            vmem((SLOTS, HEAD_DIM), F32),
            vmem((SLOTS, HEAD_DIM), F32),
        ],
        name="attention",
    )(
        meta,
        jnp.asarray(rep, BF16),
        jnp.asarray(pick, BF16),
        jnp.asarray(base, BF16),
        pattern,
        jnp.asarray(hidden, BF16),
        arrived,
        arrived,
        arrived,
        arrived,
    )


def combine_kernel(
    slots_ref,
    dk_ref,
    o_ref,
    dq_ref,
    dv_ref,
    dk_home,
    o_home,
    dq_home,
    dv_home,
    held,
    placing,
    sending,
    d_send,
    d_recv,
    z_send,
    z_recv,
):
    y, z, core = place()
    d = y * 2 + core
    sources = (dk_ref, o_ref, dq_ref, dv_ref)
    homes = (dk_home, o_home, dq_home, dv_home)
    greet(y, z, core, d)

    def d_copy(a, k):
        to = lax.rem(d + k, ND)
        return pltpu.make_async_remote_copy(
            src_ref=sources[a].at[to],
            dst_ref=held.at[a, d],
            send_sem=d_send.at[a, to],
            recv_sem=d_recv.at[a, d],
            device_id={"seq": along_d(to, z)},
            device_id_type=MESH,
        )

    def d_arrival(a, k):
        came = lax.rem(d + k, ND)
        return pltpu.make_async_remote_copy(
            src_ref=held.at[a, came],
            dst_ref=held.at[a, came],
            send_sem=d_send.at[a, came],
            recv_sem=d_recv.at[a, came],
            device_id={"seq": along_d(came, z)},
            device_id_type=MESH,
        )

    def z_copy(a, k):
        to = lax.rem(z + k, NZ)
        return pltpu.make_async_remote_copy(
            src_ref=sending.at[a, to],
            dst_ref=homes[a].at[:, head_columns(z)],
            send_sem=z_send.at[a, to],
            recv_sem=z_recv.at[a, z],
            device_id={"seq": along_z(y, core, to)},
            device_id_type=MESH,
        )

    def z_arrival(a, k):
        came = lax.rem(z + k, NZ)
        return pltpu.make_async_remote_copy(
            src_ref=sending.at[a, came],
            dst_ref=homes[a].at[:, head_columns(came)],
            send_sem=z_send.at[a, came],
            recv_sem=z_recv.at[a, came],
            device_id={"seq": along_z(y, core, came)},
            device_id_type=MESH,
        )

    def z_own(a):
        return pltpu.make_async_copy(
            sending.at[a, z], homes[a].at[:, head_columns(z)], z_recv.at[a, z]
        )

    def each(first, body):
        def step(k, carry):
            body(k)
            return carry

        lax.fori_loop(first, 8, step, 0)

    for a in range(4):
        each(1, lambda k, a=a: d_copy(a, k).start())
        pltpu.make_async_copy(sources[a].at[d], held.at[a, d], d_recv.at[a, d]).start()

    across = lax.broadcasted_iota(jnp.int32, (T_DEV, T_DEV), 1)
    down = lax.broadcasted_iota(jnp.int32, (T_DEV, T_DEV), 0)
    eye = jnp.where(down == across, 1.0, 0.0).astype(BF16)

    def build(zz, carry):
        there = expander(slots_ref[zz], lax.rem(zz, 2))
        placing[zz] = contract_last(eye, there).astype(BF16)
        return carry

    lax.fori_loop(0, NZ, build, 0)

    for a in range(4):
        pltpu.make_async_copy(held.at[a, d], held.at[a, d], d_recv.at[a, d]).wait()
        each(1, lambda k, a=a: d_arrival(a, k).wait_recv())

        def gather(k, a=a):
            to = lax.rem(z + k, NZ)
            rows = held[a, :, to // 2].reshape(ROWS, HEAD_DIM)
            found = jnp.dot(placing[to], rows, preferred_element_type=F32)
            sending[a, to] = found.astype(BF16)

        def gather_send(k, a=a):
            gather(k)
            z_copy(a, k).start()

        each(1, gather_send)
        gather(0)
        z_own(a).start()

    for a in range(4):
        z_own(a).wait()

        def one(k, a=a):
            z_arrival(a, k).wait_recv()
            z_arrival(a, k).wait_send()
            d_arrival(a, k).wait_send()

        each(1, one)


def combine(slots, dk, o, dq, dv):
    any_space = pl.BlockSpec(memory_space=pl.ANY)
    dma = pltpu.SemaphoreType.DMA
    home = jax.ShapeDtypeStruct((T_DEV, NZ * HEAD_DIM), BF16)
    return pl.pallas_call(
        combine_kernel,
        out_shape=(home,) * 4,
        in_specs=[pl.BlockSpec(memory_space=pltpu.VMEM)] + [any_space] * 4,
        out_specs=(any_space,) * 4,
        scratch_shapes=[
            pltpu.VMEM((4, ND, NZ // 2, 2, PAIR, HEAD_DIM), BF16),
            pltpu.VMEM((NZ, T_DEV, ROWS), BF16),
            pltpu.VMEM((4, NZ, T_DEV, HEAD_DIM), BF16),
            dma((4, ND)),
            dma((4, ND)),
            dma((4, NZ)),
            dma((4, NZ)),
        ],
        compiler_params=pltpu.CompilerParams(collective_id=1, has_side_effects=True),
        name="combine",
    )(slots, dk, o, dq, dv)


def per_device(queries, key_vectors, values, cotangent, cluster, block_pattern):
    me = lax.axis_index("seq")
    d = (me // (2 * NZ)) * 2 + me % 2
    key_float = key_vectors.astype(F32)
    square_sum = lax.psum(jnp.sum(key_float * key_float, axis=1), "head")
    key_rms = jnp.sqrt(square_sum / (HEADS * HEAD_DIM) + EPSILON)[:, None]
    normed_float = key_float / key_rms
    normed = normed_float.astype(BF16)
    ids = cluster[:, 0]
    token = jnp.arange(T_DEV, dtype=jnp.int32)
    earlier = (ids[:, None] == ids[None, :]) & (token[:, None] < token[None, :])
    rank = jnp.sum(earlier.astype(jnp.int32), axis=0)
    slot = ids * PAIR + rank
    slot_row = jnp.pad(slot, (0, 256 - T_DEV), constant_values=-1).reshape(1, 256)
    meta_slot = (ids // 2) * 128 + (ids % 2) * CAP + rank
    spots = jnp.arange(ND * 128, dtype=jnp.int32)
    hit = meta_slot[:, None] == spots[None, :]
    meta_row = jnp.sum(jnp.where(hit, (token + 1).astype(F32)[:, None], 0.0), axis=0)
    arrived, meta, slots = dispatch(
        slot_row, meta_row.reshape(1, ND * 128), values, cotangent, queries, normed
    )
    pattern = lax.dynamic_slice_in_dim(block_pattern, 2 * d, 2, 0)
    blocks = pattern.shape[1]
    pattern = jnp.where(pattern == 1, 0.0, -BIG)
    pattern = jnp.pad(pattern, ((0, 0), (0, 0), (0, 1)), constant_values=-BIG)
    pattern = jnp.pad(pattern, ((0, 0), (0, 128 - blocks), (0, 127 - blocks))).astype(BF16)
    o, dq, dk, dv = attention(meta.reshape(64, 128), pattern, arrived)
    grad_rows, attended, query_grad, value_grad = combine(slots, dk, o, dq, dv)
    grad_float = grad_rows.astype(F32)
    inner = lax.psum(jnp.sum(normed_float * grad_float, axis=1), "head")
    key_grad = (
        (grad_float - normed_float * (inner / (HEADS * HEAD_DIM))[:, None]) / key_rms
    ).astype(BF16)
    return (attended, query_grad, key_grad, value_grad)


def solution(mesh):
    in_specs = (
        P("seq", "head"),
        P("seq", "head"),
        P("seq", "head"),
        P("seq", "head"),
        P("seq", None),
        P(),
    )
    out_specs = (P("seq", "head"), P("seq", "head"), P("seq", "head"), P("seq", "head"))
    return jax.shard_map(
        per_device, mesh=mesh, in_specs=in_specs, out_specs=out_specs, check_vma=False
    )
```

time: 946 us -> 196 us (0.21)
  blocking collectives: 347 us -> 15.3 us
  waiting for transfers between devices: 256 us -> 0 us
  Pallas kernels: 0 us -> 163 us
  local copies, waits for them, and re-layouts: 128 us -> 4.85 us
  other arithmetic: 104 us -> 10.9 us
  matrix products: 70.2 us -> 0 us
  starting transfers between devices: 17 us -> 0 us
  loops' own time: 11.8 us -> 0 us
    unnamed x1 -> x0, blocking collectives: 243 us -> none
    ppermute x4 -> x0, waiting for transfers between devices: 182 us -> none  [from_partner(): return lax.ppermute(value, axis, pairs)]
    pallas_call x0 -> x3, Pallas kernels: none -> 163 us  [the longest x1 60 us: dispatch(): pl.pallas_call(dispatch_kernel, out_shape=(jax.ShapeDtypeStruct((4, ND, N...]
    all_to_all x1 -> x0, blocking collectives: 87.8 us -> none  [dispatch_rows(): lax.all_to_all(outgoing, 'seq', split_axis=1, concat_axis=1, tiled=True)]
    all_to_all x1 -> x0, waiting for transfers between devices: 73.4 us -> none  [combine_rows(): lax.all_to_all(outgoing, 'seq', split_axis=1, concat_axis=1, tiled=True)]
    dot_general x50 -> x0, matrix products: 70.2 us -> none  [the longest x16 29.4 us: contract_last(): lax.dot_general(left_side, right_side, (((1,), (1,)), ((), ())), preferre...]
    select_n x7 -> x0, other arithmetic: 60.2 us -> none  [the longest x2 47.3 us: collect(): jnp.where(lower_side, jnp.concatenate([combined, partner_piece], along),...]
    dynamic_update_slice x8 -> x0, local copies, waits for them, and re-layouts: 53.5 us -> none  [one_head(): lax.dynamic_update_slice_in_dim(side_acc, jnp.stack([key_part, value_part...]
  transfers between devices with their start and end apart: 5 -> 0, of which waited for: 4 -> 0; matrix products, arithmetic and copies ran while one was open for 2% -> 0% of each run, Pallas kernels for 0% -> 0%
where the time goes in v1:
time: 196 us; the launch traced here: 195 us
  Pallas kernels  163 us (83%)
  blocking collectives  15.3 us (8%)
  other arithmetic  10.9 us (6%)
  local copies, waits for them, and re-layouts  4.85 us (2%)
    pallas_call x1, Pallas kernels, dispatch(): pl.pallas_call(dispatch_kernel, out_shape=(jax.ShapeDtypeStruct((4, ND, N...  60 us
    pallas_call x1, Pallas kernels, combine(): pl.pallas_call(combine_kernel, out_shape=(home,) * 4, in_specs=[pl.BlockS...  54.1 us
    pallas_call x1, Pallas kernels, attention(): pl.pallas_call(functools.partial(attention_kernel, HEAD_DIM ** (-0.5)), o...  49.1 us
    psum x1, blocking collectives, per_device(): square_sum = lax.psum(jnp.sum(key_float * key_float, axis=1), 'head')  9.29 us
    psum x1, blocking collectives, per_device(): inner = lax.psum(jnp.sum(normed_float * grad_float, axis=1), 'head')  6.04 us
    unnamed x7, local copies, waits for them, and re-layouts  4.29 us

profile of v1, /device:TPU:1, one launch (start us, length us, event | category | flops | bytes accessed | tf_op | source)
XLA Modules:
  0.0 195.0 jit_solution(13249932878965399743)
XLA Ops:
  0.7 0.9 convert_reduce_fusion
  1.5 0.7 fusion.10
  2.2 0.7 multiply_add_fusion
  2.9 0.6 pad.14
  3.5 1.2 fusion
  4.6 9.3 %psum.14 = f32[192]{0:T(256)S(1)} all-reduce(f32[192]{0:T(256)S(1)} %fusion), channel_id=1, replica_groups=mesh['seq'=64,'head'=4] {'head'}, use_global_device_ids=true, to_apply=%region_3.4 | all-reduce | flops 192 | bytes 1536 | tf_op jit(solution)/shard_map/psum | solution.py:683
  13.9 0.8 select_reduce_fusion
  14.7 0.9 select_convert_fusion
  15.6 0.6 fusion.7.pattern_ref
  16.2 1.9 fusion.11.k_ref
  18.1 60.0 %dispatch.1 = (bf16[4,8,4,2,48,128]{5,4,3,2,1,0:T(8,128)(2,1)}, f32[8,8,1,128]{3,2,1,0:T(1,128)}, s32[8,1,256]{2,1,0:T(1,128)}) custom-call(s32[1,256]{1,0:T(1,128)} %bitcast.12, f32[1,1024]{1,0:T(1,128)} %bitcast.7, bf16[192,1024]{1,0:T(8,128)(2,1)} %v_ref.1, bf16[192,1024]{1,0:T(8,128)(2,1)} %g_ref.1, bf16[192,1024]{1,0:T(8,128)(2,1)} %q_ref.1, ...), custom_call_target="tpu_custom_call" | custom-call | tf_op jit(solution)/shard_map/dispatch/pallas_call | solution.py:310
  78.1 49.1 %attention.1 = (bf16[8,4,2,48,128]{4,3,2,1,0:T(8,128)(2,1)}, bf16[8,4,2,48,128]{4,3,2,1,0:T(8,128)(2,1)}, bf16[8,4,2,48,128]{4,3,2,1,0:T(8,128)(2,1)}, bf16[8,4,2,48,128]{4,3,2,1,0:T(8,128)(2,1)}) custom-call(f32[64,128]{1,0:T(8,128)} %bitcast.6, bf16[1536,64]{1,0:T(8,128)(2,1)} %constant.85.clone.rep_ref, bf16[2,1536,128]{2,1,0:T(8,128)(2,1)} %constant.86.clone.pick_ref, ...), custom_call_target="tpu_custom_call" | custom-call | tf_op jit(solution)/shard_map/attention/pallas_call | solution.py:497
  127.2 0.0 copy-start
  127.2 54.1 %combine.1 = (bf16[192,1024]{1,0:T(8,128)(2,1)}, bf16[192,1024]{1,0:T(8,128)(2,1)}, bf16[192,1024]{1,0:T(8,128)(2,1)}, bf16[192,1024]{1,0:T(8,128)(2,1)}) custom-call(s32[8,1,256]{2,1,0:T(1,128)} %get-tuple-element.15.slots_ref, bf16[8,4,2,48,128]{4,3,2,1,0:T(8,128)(2,1)} %get-tuple-element.18.dk_ref, bf16[8,4,2,48,128]{4,3,2,1,0:T(8,128)(2,1)} %get-tuple-element.19.o_ref, ...), custom_call_target="tpu_custom_call" | custom-call | tf_op jit(solution)/shard_map/combine/pallas_call | solution.py:660
  181.3 0.0 copy-start.1
  181.3 0.0 copy-done
  181.3 1.3 fusion.1
  182.7 6.0 %psum.15 = f32[192]{0:T(256)S(1)} all-reduce(f32[192]{0:T(256)S(1)} %fusion.1), channel_id=1, replica_groups=mesh['seq'=64,'head'=4] {'head'}, use_global_device_ids=true, to_apply=%region_5.6 | all-reduce | flops 192 | bytes 1536 | tf_op jit(solution)/shard_map/psum | solution.py:708
  188.7 2.0 %fusion.3 = bf16[192,1024]{1,0:T(8,128)(2,1)} fusion(bf16[192,1024]{1,0:T(8,128)(2,1)} %get-tuple-element.24, f32[192]{0:T(256)S(1)} %broadcast_multiply_fusion, f32[192]{0:T(256)S(1)} %add_sqrt_fusion, bf16[192,1024]{1,0:T(8,128)(2,1)S(1)} %copy-done), kind=kLoop, calls=%fused_computation.7 | loop fusion | flops 1376256 | bytes 1181184 | tf_op jit(solution)/shard_map/convert_element_type | solution.py:711
  190.7 1.8 copy.17
  192.5 1.8 copy.18
  194.2 0.0 copy-done.1
  194.2 0.7 copy.19
  (3 shorter events, 0.0 us)
Async XLA Ops:
  127.2 54.2 %copy-start = (bf16[192,1024]{1,0:T(8,128)(2,1)S(1)}, bf16[192,1024]{1,0:T(8,128)(2,1)}, u32[]{:S(2)}) copy-start(bf16[192,1024]{1,0:T(8,128)(2,1)} %param.11) | copy-start | bytes 1179652
  181.3 12.9 %copy-start.1 = (bf16[192,1024]{1,0:T(8,128)(2,1)S(1)}, bf16[192,1024]{1,0:T(8,128)(2,1)}, u32[]{:S(2)}) copy-start(bf16[192,1024]{1,0:T(8,128)(2,1)} %get-tuple-element.33) | copy-start | bytes 1179652

commit v2 on v1

--- a/solution.py
+++ b/solution.py
@@ -21,7 +21,6 @@
 ROWS = GROUPS * PAIR
 SLOTS = 64 * CAP
 QB = SLOTS // 4
-CH = 128
 BIG = 1e30
 MESH = pl.DeviceIdType.MESH
 F32 = jnp.float32
@@ -101,6 +100,8 @@
     held,
     placing,
     sending,
+    landed,
+    out_sem,
     small_send,
     small_recv,
     meta_send,
@@ -177,7 +178,7 @@
         to = lax.rem(d + k, ND)
         return pltpu.make_async_remote_copy(
             src_ref=sending.at[a, :, to],
-            dst_ref=out_ref.at[a, d],
+            dst_ref=landed.at[a, d],
             send_sem=d_send.at[a, to],
             recv_sem=d_recv.at[a, d],
             device_id={"seq": along_d(to, z)},
@@ -187,8 +188,8 @@
     def d_arrival(a, k):
         came = lax.rem(d + k, ND)
         return pltpu.make_async_remote_copy(
-            src_ref=out_ref.at[a, came],
-            dst_ref=out_ref.at[a, came],
+            src_ref=landed.at[a, came],
+            dst_ref=landed.at[a, came],
             send_sem=d_send.at[a, came],
             recv_sem=d_recv.at[a, came],
             device_id={"seq": along_d(came, z)},
@@ -196,7 +197,10 @@
         )
 
     def d_own(a):
-        return pltpu.make_async_copy(sending.at[a, :, d], out_ref.at[a, d], d_recv.at[a, d])
+        return pltpu.make_async_copy(sending.at[a, :, d], landed.at[a, d], d_recv.at[a, d])
+
+    def put_out(a):
+        return pltpu.make_async_copy(landed.at[a], out_ref.at[a], out_sem.at[a])
 
     def meta_copy(k):
         to = lax.rem(d + k, ND)
@@ -281,10 +285,11 @@
     lax.fori_loop(0, 4, expand, 0)
 
     def finish(a, carry):
-        pltpu.make_async_copy(out_ref.at[a, d], out_ref.at[a, d], d_recv.at[a, d]).wait()
+        d_own(a).wait()
+        each(1, lambda k: d_arrival(a, k).wait_recv())
+        put_out(a).start()
 
         def one(k):
-            d_arrival(a, k).wait_recv()
             d_arrival(a, k).wait_send()
             z_arrival(a, k).wait_send()
 
@@ -292,6 +297,12 @@
         return carry
 
     lax.fori_loop(0, 4, finish, 0)
+
+    def close(a, carry):
+        put_out(a).wait()
+        return carry
+
+    lax.fori_loop(0, 4, close, 0)
     keep_slots.wait()
     meta_own().wait()
 
@@ -322,6 +333,8 @@
             pltpu.VMEM((4, NZ, T_DEV, HEAD_DIM), BF16),
             pltpu.VMEM((NZ, ROWS, T_DEV), BF16),
             pltpu.VMEM((4, NZ // 2, ND, 2, PAIR, HEAD_DIM), BF16),
+            pltpu.VMEM((4, ND, NZ // 2, 2, PAIR, HEAD_DIM), BF16),
+            dma((4,)),
             dma((2, NZ)),
             dma((2, NZ)),
             dma((ND,)),
@@ -363,8 +376,6 @@
     prob_grads,
     probs,
     score_grads,
-    key_acc,
-    value_acc,
 ):
     flat = (SLOTS, HEAD_DIM)
     numbers = jnp.dot(rep_ref[...], meta_ref[...].astype(BF16), preferred_element_type=F32)
@@ -390,75 +401,58 @@
     value_t[...] = contract_last(small_eye, values[...]).astype(BF16)
     turn = score_scale * 1.4426950408889634
 
-    def chunk(j, start=0):
-        return pl.ds(pl.multiple_of(start + j * CH, CH), CH)
+    shape = (2, NZ // 2, PAIR, HEAD_DIM)
 
     def fold(piece, op):
-        return op(piece.reshape(CH // 8, 8, QB), axis=0)
-
-    for i in (3, 2, 1, 0):
+        return op(piece.reshape(QB // 8, 8, QB), axis=0)
+
+    def part(j):
+        return pl.ds(QB * j, QB)
+
+    for i in range(4):
         span = QB * (i + 1)
-        query_rows = queries[QB * i : span, :]
-        grad_rows = grads[QB * i : span, :]
-
-        def full_scores(j, running):
-            piece = contract_last(keys[chunk(j), :], query_rows)
-            scores[chunk(j), :] = piece
-            return jnp.maximum(running, fold(piece, jnp.max))
-
-        def edge_scores(j, running):
-            piece = contract_last(keys[chunk(j, QB * i), :], query_rows)
-            piece += order_ref[chunk(j), :].astype(F32)
-            scores[chunk(j, QB * i), :] = piece
-            return jnp.maximum(running, fold(piece, jnp.max))
-
-        top = jnp.full((8, QB), -3e38, F32)
-        if i:
-            top = lax.fori_loop(0, 3 * i, full_scores, top)
-        top = lax.fori_loop(0, 3, edge_scores, top)
+        query_rows = queries[part(i), :]
+        grad_rows = grads[part(i), :]
+        side = i % 2
+        top = None
+        for j in range(i + 1):
+            piece = contract_last(keys[part(j), :], query_rows)
+            if j == i:
+                piece += order_ref[...].astype(F32)
+            scores[side, part(j), :] = piece
+            most = fold(piece, jnp.max)
+            top = most if top is None else jnp.maximum(top, most)
         top = jnp.max(top, axis=0, keepdims=True)
-
-        def weigh(j, running):
-            total, delta = running
-            weights = jnp.exp2((scores[chunk(j), :] - top) * turn)
-            scores[chunk(j), :] = weights
-            terms = contract_last(values[chunk(j), :], grad_rows)
-            prob_grads[chunk(j), :] = terms
-            return (total + fold(weights, jnp.sum), delta + fold(weights * terms, jnp.sum))
-
-        zero = jnp.zeros((8, QB), F32)
-        total, delta = lax.fori_loop(0, 3 * (i + 1), weigh, (zero, zero))
+        total = jnp.zeros((8, QB), F32)
+        delta = jnp.zeros((8, QB), F32)
+        for j in range(i + 1):
+            terms = contract_last(values[part(j), :], grad_rows)
+            prob_grads[side, part(j), :] = terms
+            weights = jnp.exp2((scores[side, part(j), :] - top) * turn)
+            scores[side, part(j), :] = weights
+            total += fold(weights, jnp.sum)
+            delta += fold(weights * terms, jnp.sum)
         inverse = 1.0 / jnp.maximum(jnp.sum(total, axis=0, keepdims=True), 1.0)
         delta = jnp.sum(delta, axis=0, keepdims=True) * inverse
-
-        def settle(j, carry):
-            shares = scores[chunk(j), :] * inverse
-            half = shares.astype(BF16)
-            probs[chunk(j), :] = half
-            slopes = (shares * (prob_grads[chunk(j), :] - delta)).astype(BF16)
-            score_grads[chunk(j), :] = slopes
-            value_part = jnp.dot(half, grad_rows, preferred_element_type=F32)
-            key_part = jnp.dot(slopes, query_rows[:, :HEAD_DIM], preferred_element_type=F32)
-            if i == 3:
-                value_acc[chunk(j), :] = value_part
-                key_acc[chunk(j), :] = key_part
-            else:
-                value_acc[chunk(j), :] += value_part
-                key_acc[chunk(j), :] += key_part
-            return carry
-
-        lax.fori_loop(0, 3 * (i + 1), settle, 0)
-        shape = (2, NZ // 2, PAIR, HEAD_DIM)
-        attended_t = jnp.dot(value_t[:, :span], probs[:span, :], preferred_element_type=F32)
+        for j in range(i + 1):
+            shares = scores[side, part(j), :] * inverse
+            probs[part(j), part(i)] = shares.astype(BF16)
+            slopes = shares * (prob_grads[side, part(j), :] - delta)
+            score_grads[part(j), part(i)] = slopes.astype(BF16)
+        attended_t = jnp.dot(value_t[:, :span], probs[:span, part(i)], preferred_element_type=F32)
         attended = contract_last(eye, attended_t.astype(BF16))
         o_ref[2 * i : 2 * i + 2] = attended.astype(BF16).reshape(shape)
-        query_t = jnp.dot(key_t[:, :span], score_grads[:span, :], preferred_element_type=F32)
+        query_t = jnp.dot(key_t[:, :span], score_grads[:span, part(i)], preferred_element_type=F32)
         query_grad = contract_last(eye, (query_t * score_scale).astype(BF16))
         dq_ref[2 * i : 2 * i + 2] = query_grad.astype(BF16).reshape(shape)
 
-    whole = (ND, NZ // 2, PAIR, HEAD_DIM)
-    dk_ref[...] = (key_acc[...] * score_scale).astype(BF16).reshape(whole)
-    dv_ref[...] = value_acc[...].astype(BF16).reshape(whole)
+    for j in range(4):
+        first = QB * j
+        slopes = score_grads[part(j), first:]
+        key_grad = jnp.dot(slopes, queries[first:, :HEAD_DIM], preferred_element_type=F32)
+        dk_ref[2 * j : 2 * j + 2] = (key_grad * score_scale).astype(BF16).reshape(shape)
+        value_grad = jnp.dot(probs[part(j), first:], grads[first:, :], preferred_element_type=F32)
+        dv_ref[2 * j : 2 * j + 2] = value_grad.astype(BF16).reshape(shape)
 
 
 def slot_tables():
@@ -507,12 +501,10 @@
             vmem((SLOTS, HEAD_DIM), BF16),
             vmem((HEAD_DIM, SLOTS), BF16),
             vmem((HEAD_DIM, SLOTS), BF16),
-            vmem((SLOTS, QB), F32),
-            vmem((SLOTS, QB), F32),
-            vmem((SLOTS, QB), BF16),
-            vmem((SLOTS, QB), BF16),
-            vmem((SLOTS, HEAD_DIM), F32),
-            vmem((SLOTS, HEAD_DIM), F32),
+            vmem((2, SLOTS, QB), F32),
+            vmem((2, SLOTS, QB), F32),
+            vmem((SLOTS, SLOTS), BF16),
+            vmem((SLOTS, SLOTS), BF16),
         ],
         name="attention",
     )(
@@ -542,6 +534,8 @@
     held,
     placing,
     sending,
+    landed,
+    out_sem,
     d_send,
     d_recv,
     z_send,
@@ -579,7 +573,7 @@
         to = lax.rem(z + k, NZ)
         return pltpu.make_async_remote_copy(
             src_ref=sending.at[a, to],
-            dst_ref=homes[a].at[:, head_columns(z)],
+            dst_ref=landed.at[a, :, head_columns(z)],
             send_sem=z_send.at[a, to],
             recv_sem=z_recv.at[a, z],
             device_id={"seq": along_z(y, core, to)},
@@ -590,7 +584,7 @@
         came = lax.rem(z + k, NZ)
         return pltpu.make_async_remote_copy(
             src_ref=sending.at[a, came],
-            dst_ref=homes[a].at[:, head_columns(came)],
+            dst_ref=landed.at[a, :, head_columns(came)],
             send_sem=z_send.at[a, came],
             recv_sem=z_recv.at[a, came],
             device_id={"seq": along_z(y, core, came)},
@@ -599,7 +593,7 @@
 
     def z_own(a):
         return pltpu.make_async_copy(
-            sending.at[a, z], homes[a].at[:, head_columns(z)], z_recv.at[a, z]
+            sending.at[a, z], landed.at[a, :, head_columns(z)], z_recv.at[a, z]
         )
 
     def each(first, body):
@@ -642,15 +636,22 @@
         gather(0)
         z_own(a).start()
 
+    def put_out(a):
+        return pltpu.make_async_copy(landed.at[a], homes[a], out_sem.at[a])
+
     for a in range(4):
         z_own(a).wait()
+        each(1, lambda k, a=a: z_arrival(a, k).wait_recv())
+        put_out(a).start()
+
+    for a in range(4):
 
         def one(k, a=a):
-            z_arrival(a, k).wait_recv()
             z_arrival(a, k).wait_send()
             d_arrival(a, k).wait_send()
 
         each(1, one)
+        put_out(a).wait()
 
 
 def combine(slots, dk, o, dq, dv):
@@ -666,6 +667,8 @@
             pltpu.VMEM((4, ND, NZ // 2, 2, PAIR, HEAD_DIM), BF16),
             pltpu.VMEM((NZ, T_DEV, ROWS), BF16),
             pltpu.VMEM((4, NZ, T_DEV, HEAD_DIM), BF16),
+            pltpu.VMEM((4, T_DEV, NZ * HEAD_DIM), BF16),
+            dma((4,)),
             dma((4, ND)),
             dma((4, ND)),
             dma((4, NZ)),

time: 196 us -> 170 us (0.87)
  Pallas kernels: 163 us -> 137 us
    pallas_call x1, Pallas kernels: 49.1 us -> 21.8 us  [attention(): pl.pallas_call(functools.partial(attention_kernel, HEAD_DIM ** (-0.5)), o...]
where the time goes in v2:
time: 170 us; the launch traced here: 169 us
  Pallas kernels  137 us (81%)
  blocking collectives  15.3 us (9%)
  other arithmetic  10.9 us (6%)
  local copies, waits for them, and re-layouts  4.85 us (3%)
    pallas_call x1, Pallas kernels, dispatch(): pl.pallas_call(dispatch_kernel, out_shape=(jax.ShapeDtypeStruct((4, ND, N...  60.7 us
    pallas_call x1, Pallas kernels, combine(): pl.pallas_call(combine_kernel, out_shape=(home,) * 4, in_specs=[pl.BlockS...  54.9 us
    pallas_call x1, Pallas kernels, attention(): pl.pallas_call(functools.partial(attention_kernel, HEAD_DIM ** (-0.5)), o...  21.8 us
    psum x1, blocking collectives, per_device(): square_sum = lax.psum(jnp.sum(key_float * key_float, axis=1), 'head')  9.29 us
    psum x1, blocking collectives, per_device(): inner = lax.psum(jnp.sum(normed_float * grad_float, axis=1), 'head')  6 us
    unnamed x7, local copies, waits for them, and re-layouts  4.29 us

profile of v2, /device:TPU:1, one launch (start us, length us, event | category | flops | bytes accessed | tf_op | source)
XLA Modules:
  0.0 169.2 jit_solution(18428031603319248024)
XLA Ops:
  0.7 0.9 convert_reduce_fusion
  1.5 0.7 fusion.10
  2.2 0.7 multiply_add_fusion
  2.9 0.6 pad.14
  3.5 1.2 fusion
  4.6 9.3 %psum.14 = f32[192]{0:T(256)S(1)} all-reduce(f32[192]{0:T(256)S(1)} %fusion), channel_id=1, replica_groups=mesh['seq'=64,'head'=4] {'head'}, use_global_device_ids=true, to_apply=%region_3.4 | all-reduce | flops 192 | bytes 1536 | tf_op jit(solution)/shard_map/psum | solution.py:686
  13.9 0.8 select_reduce_fusion
  14.7 0.9 select_convert_fusion
  15.6 0.6 fusion.7.pattern_ref
  16.2 1.9 %fusion.11.k_ref = bf16[192,1024]{1,0:T(8,128)(2,1)} fusion(f32[192]{0:T(256)S(1)} %add_sqrt_fusion, bf16[192,1024]{1,0:T(8,128)(2,1)} %param.11), kind=kLoop, calls=%fused_computation.32 | loop fusion | flops 589824 | bytes 787200 | tf_op jit(solution)/shard_map/convert_element_type | solution.py:689
  18.1 60.7 %dispatch.1 = (bf16[4,8,4,2,48,128]{5,4,3,2,1,0:T(8,128)(2,1)}, f32[8,8,1,128]{3,2,1,0:T(1,128)}, s32[8,1,256]{2,1,0:T(1,128)}) custom-call(s32[1,256]{1,0:T(1,128)} %bitcast.12, f32[1,1024]{1,0:T(1,128)} %bitcast.7, bf16[192,1024]{1,0:T(8,128)(2,1)} %v_ref.1, bf16[192,1024]{1,0:T(8,128)(2,1)} %g_ref.1, bf16[192,1024]{1,0:T(8,128)(2,1)} %q_ref.1, ...), custom_call_target="tpu_custom_call" | custom-call | tf_op jit(solution)/shard_map/dispatch/pallas_call | solution.py:321
  78.9 21.8 %attention.1 = (bf16[8,4,2,48,128]{4,3,2,1,0:T(8,128)(2,1)}, bf16[8,4,2,48,128]{4,3,2,1,0:T(8,128)(2,1)}, bf16[8,4,2,48,128]{4,3,2,1,0:T(8,128)(2,1)}, bf16[8,4,2,48,128]{4,3,2,1,0:T(8,128)(2,1)}) custom-call(f32[64,128]{1,0:T(8,128)} %bitcast.6, bf16[1536,64]{1,0:T(8,128)(2,1)} %constant.85.clone.rep_ref, bf16[2,1536,128]{2,1,0:T(8,128)(2,1)} %constant.86.clone.pick_ref, ...), custom_call_target="tpu_custom_call" | custom-call | tf_op jit(solution)/shard_map/attention/pallas_call | solution.py:491
  100.6 0.0 copy-start
  100.6 54.9 %combine.1 = (bf16[192,1024]{1,0:T(8,128)(2,1)}, bf16[192,1024]{1,0:T(8,128)(2,1)}, bf16[192,1024]{1,0:T(8,128)(2,1)}, bf16[192,1024]{1,0:T(8,128)(2,1)}) custom-call(s32[8,1,256]{2,1,0:T(1,128)} %get-tuple-element.15.slots_ref, bf16[8,4,2,48,128]{4,3,2,1,0:T(8,128)(2,1)} %get-tuple-element.18.dk_ref, bf16[8,4,2,48,128]{4,3,2,1,0:T(8,128)(2,1)} %get-tuple-element.19.o_ref, ...), custom_call_target="tpu_custom_call" | custom-call | tf_op jit(solution)/shard_map/combine/pallas_call | solution.py:661
  155.6 0.0 copy-start.1
  155.6 0.0 copy-done
  155.6 1.3 fusion.1
  156.9 6.0 %psum.15 = f32[192]{0:T(256)S(1)} all-reduce(f32[192]{0:T(256)S(1)} %fusion.1), channel_id=1, replica_groups=mesh['seq'=64,'head'=4] {'head'}, use_global_device_ids=true, to_apply=%region_5.6 | all-reduce | flops 192 | bytes 1536 | tf_op jit(solution)/shard_map/psum | solution.py:711
  162.9 2.0 %fusion.3 = bf16[192,1024]{1,0:T(8,128)(2,1)} fusion(bf16[192,1024]{1,0:T(8,128)(2,1)} %get-tuple-element.24, f32[192]{0:T(256)S(1)} %broadcast_multiply_fusion, f32[192]{0:T(256)S(1)} %add_sqrt_fusion, bf16[192,1024]{1,0:T(8,128)(2,1)S(1)} %copy-done), kind=kLoop, calls=%fused_computation.7 | loop fusion | flops 1376256 | bytes 1181184 | tf_op jit(solution)/shard_map/convert_element_type | solution.py:714
  164.9 1.8 %copy.17 = bf16[192,1024]{1,0:T(8,128)(2,1)} copy(bf16[192,1024]{1,0:T(8,128)(2,1)} %get-tuple-element.30) | data formatting | bytes 786432
  166.7 1.8 %copy.18 = bf16[192,1024]{1,0:T(8,128)(2,1)} copy(bf16[192,1024]{1,0:T(8,128)(2,1)} %get-tuple-element.31) | data formatting | bytes 786432
  168.5 0.0 copy-done.1
  168.5 0.7 copy.19
  (3 shorter events, 0.0 us)
Async XLA Ops:
  100.6 55.0 %copy-start = (bf16[192,1024]{1,0:T(8,128)(2,1)S(1)}, bf16[192,1024]{1,0:T(8,128)(2,1)}, u32[]{:S(2)}) copy-start(bf16[192,1024]{1,0:T(8,128)(2,1)} %param.11) | copy-start | bytes 1179652
  155.6 12.9 %copy-start.1 = (bf16[192,1024]{1,0:T(8,128)(2,1)S(1)}, bf16[192,1024]{1,0:T(8,128)(2,1)}, u32[]{:S(2)}) copy-start(bf16[192,1024]{1,0:T(8,128)(2,1)} %get-tuple-element.33) | copy-start | bytes 1179652

commit v3 on v2

--- a/solution.py
+++ b/solution.py
@@ -15,6 +15,7 @@
 CAP = 24
 NZ = 8
 ND = 8
+NX = 4
 T_DEV = 192
 GROUPS = 16
 PAIR = 2 * CAP
@@ -49,7 +50,7 @@
     return ((d // 2) * NZ + z) * 2 + lax.rem(d, 2)
 
 
-def greet(y, z, core, d):
+def greet(y, z, core, d, x):
     barrier = pltpu.get_barrier_semaphore()
 
     def signal(k, carry):
@@ -68,7 +69,15 @@
         return carry
 
     lax.fori_loop(1, 8, signal, 0)
-    pl.semaphore_wait(barrier, 14)
+
+    def signal_x(k, carry):
+        pl.semaphore_signal(
+            barrier, inc=1, device_id={"head": lax.rem(x + k, NX)}, device_id_type=MESH
+        )
+        return carry
+
+    lax.fori_loop(1, NX, signal_x, 0)
+    return barrier
 
 
 def head_columns(z):
@@ -85,18 +94,60 @@
     return jnp.where(hit, 1.0, 0.0).astype(BF16)
 
 
+def each(first, body, last=8):
+    def step(k, carry):
+        body(k)
+        return carry
+
+    lax.fori_loop(first, last, step, 0)
+
+
+def x_copies(x, parts, send, recv):
+    def copy(k):
+        to = lax.rem(x + k, NX)
+        return pltpu.make_async_remote_copy(
+            src_ref=parts.at[x],
+            dst_ref=parts.at[x],
+            send_sem=send.at[to],
+            recv_sem=recv.at[x],
+            device_id={"head": to},
+            device_id_type=MESH,
+        )
+
+    def arrival(k):
+        came = lax.rem(x + k, NX)
+        return pltpu.make_async_remote_copy(
+            src_ref=parts.at[came],
+            dst_ref=parts.at[came],
+            send_sem=send.at[came],
+            recv_sem=recv.at[came],
+            device_id={"head": came},
+            device_id_type=MESH,
+        )
+
+    return copy, arrival
+
+
+def lanes_summed(wide):
+    return sum(wide[:, HEAD_DIM * j : HEAD_DIM * (j + 1)] for j in range(NZ))
+
+
 def dispatch_kernel(
-    slot_ref,
-    meta_ref,
+    ids_ref,
+    key_ref,
     v_ref,
     g_ref,
     q_ref,
-    k_ref,
     out_ref,
     meta_out,
     slots_out,
+    rms_out,
+    own_slot,
+    own_meta,
     slots,
     metas,
+    parts,
+    normed,
     held,
     placing,
     sending,
@@ -106,6 +157,8 @@
     small_recv,
     meta_send,
     meta_recv,
+    x_send,
+    x_recv,
     z_send,
     z_recv,
     d_send,
@@ -114,18 +167,35 @@
 ):
     y, z, core = place()
     d = y * 2 + core
-    sources = (v_ref, g_ref, q_ref, k_ref)
-    greet(y, z, core, d)
+    x = lax.axis_index("head")
+    q0 = lax.rem(z, 4)
+    sources = (v_ref, g_ref, q_ref, normed)
+    barrier = greet(y, z, core, d, x)
+
+    key_float = key_ref[...].astype(F32)
+    parts[x] = lanes_summed(key_float * key_float)
+    ids = ids_ref[...]
+    down = lax.broadcasted_iota(jnp.int32, (T_DEV, T_DEV), 0)
+    across = lax.broadcasted_iota(jnp.int32, (T_DEV, T_DEV), 1)
+    ids_float = ids.astype(F32)
+    spread = jnp.where(down == across, ids_float, 0.0).astype(BF16)
+    column = jnp.dot(spread, jnp.ones((T_DEV, T_DEV), BF16), preferred_element_type=F32)
+    earlier = (column == ids_float) & (down < across)
+    rank = jnp.sum(jnp.where(earlier, 1.0, 0.0), axis=0, keepdims=True).astype(jnp.int32)
+    own_slot[...] = jnp.full((1, 256), -1, jnp.int32)
+    own_slot[:, :T_DEV] = ids * PAIR + rank
+    meta_slot = (ids // 2) * 128 + (ids - (ids // 2) * 2) * CAP + rank
+    spots = lax.broadcasted_iota(jnp.int32, (ND * 128, T_DEV), 0)
+    spotted = jnp.where(spots == meta_slot, 1.0, 0.0).astype(BF16)
+    numbers = (lax.broadcasted_iota(jnp.int32, (8, T_DEV), 1) + 1).astype(F32).astype(BF16)
+    own_meta[...] = contract_last(numbers, spotted)[0:1, :]
 
     def small_copy(kind, k):
         to = lax.rem(z + k, NZ)
-        if kind == 0:
-            src, dst = slot_ref, slots.at[z]
-        else:
-            src, dst = meta_ref, metas.at[z]
+        src, dst = (own_slot, slots) if kind == 0 else (own_meta, metas)
         return pltpu.make_async_remote_copy(
             src_ref=src,
-            dst_ref=dst,
+            dst_ref=dst.at[z],
             send_sem=small_send.at[kind, to],
             recv_sem=small_recv.at[kind, z],
             device_id={"seq": along_z(y, core, to)},
@@ -134,51 +204,54 @@
 
     def small_arrival(kind, k):
         came = lax.rem(z + k, NZ)
-        if kind == 0:
-            src, dst = slot_ref, slots.at[came]
-        else:
-            src, dst = meta_ref, metas.at[came]
+        src, dst = (own_slot, slots) if kind == 0 else (own_meta, metas)
         return pltpu.make_async_remote_copy(
             src_ref=src,
-            dst_ref=dst,
+            dst_ref=dst.at[came],
             send_sem=small_send.at[kind, came],
             recv_sem=small_recv.at[kind, came],
             device_id={"seq": along_z(y, core, came)},
             device_id_type=MESH,
         )
 
-    def z_copy(a, k):
+    def z_copy(a, to):
+        return pltpu.make_async_remote_copy(
+            src_ref=sources[a].at[:, head_columns(to)],
+            dst_ref=held.at[a, q0, z // 4],
+            send_sem=z_send.at[a, to],
+            recv_sem=z_recv.at[a, q0],
+            device_id={"seq": along_z(y, core, to)},
+            device_id_type=MESH,
+        )
+
+    def z_sent(a, k):
         to = lax.rem(z + k, NZ)
         return pltpu.make_async_remote_copy(
-            src_ref=sources[a].at[:, head_columns(to)],
-            dst_ref=held.at[a, z],
+            src_ref=held.at[a, q0, z // 4],
+            dst_ref=held.at[a, q0, z // 4],
             send_sem=z_send.at[a, to],
-            recv_sem=z_recv.at[a, z],
+            recv_sem=z_recv.at[a, q0],
             device_id={"seq": along_z(y, core, to)},
             device_id_type=MESH,
         )
 
-    def z_arrival(a, k):
-        came = lax.rem(z + k, NZ)
-        return pltpu.make_async_remote_copy(
-            src_ref=held.at[a, came],
-            dst_ref=held.at[a, came],
-            send_sem=z_send.at[a, came],
-            recv_sem=z_recv.at[a, came],
-            device_id={"seq": along_z(y, core, came)},
-            device_id_type=MESH,
-        )
-
-    def z_own(a):
-        return pltpu.make_async_copy(
-            sources[a].at[:, head_columns(z)], held.at[a, z], z_recv.at[a, z]
-        )
-
-    def d_copy(a, k):
+    def z_start(a):
+        pltpu.make_async_copy(
+            sources[a].at[:, head_columns(z)], held.at[a, q0, z // 4], z_recv.at[a, q0]
+        ).start()
+        z_copy(a, lax.rem(z + 4, NZ)).start()
+
+        def both(o):
+            z_copy(a, lax.rem(z + NZ - o, NZ)).start()
+            z_copy(a, lax.rem(z + 4 - o, NZ)).start()
+
+        each(1, both, 4)
+
+    def d_copy(a, q, k):
         to = lax.rem(d + k, ND)
         return pltpu.make_async_remote_copy(
-            src_ref=sending.at[a, :, to],
-            dst_ref=landed.at[a, d],
+            src_ref=sending.at[a, q, to],
+            dst_ref=landed.at[a, d, q],
             send_sem=d_send.at[a, to],
             recv_sem=d_recv.at[a, d],
             device_id={"seq": along_d(to, z)},
@@ -196,9 +269,6 @@
             device_id_type=MESH,
         )
 
-    def d_own(a):
-        return pltpu.make_async_copy(sending.at[a, :, d], landed.at[a, d], d_recv.at[a, d])
-
     def put_out(a):
         return pltpu.make_async_copy(landed.at[a], out_ref.at[a], out_sem.at[a])
 
@@ -229,27 +299,30 @@
             metas.at[:, :, pair_columns(d)], meta_out.at[d], meta_recv.at[d]
         )
 
-    def each(first, body):
-        def step(k, carry):
-            body(k)
-            return carry
-
-        lax.fori_loop(first, 8, step, 0)
+    x_copy, x_arrival = x_copies(x, parts, x_send, x_recv)
+    pl.semaphore_wait(barrier, 17)
+    each(1, lambda k: x_copy(k).start(), NX)
 
     def start_small(k):
         small_copy(0, k).start()
         small_copy(1, k).start()
 
     each(1, start_small)
-    own_slot = pltpu.make_async_copy(slot_ref, slots.at[z], small_recv.at[0, z])
-    own_meta = pltpu.make_async_copy(meta_ref, metas.at[z], small_recv.at[1, z])
-    own_slot.start()
-    own_meta.start()
-    for a in range(4):
-        z_own(a).start()
-        each(1, lambda k, a=a: z_copy(a, k).start())
-    own_slot.wait()
-    own_meta.wait()
+    own_slot_copy = pltpu.make_async_copy(own_slot, slots.at[z], small_recv.at[0, z])
+    own_meta_copy = pltpu.make_async_copy(own_meta, metas.at[z], small_recv.at[1, z])
+    own_slot_copy.start()
+    own_meta_copy.start()
+    for a in range(3):
+        z_start(a)
+    each(1, lambda k: x_arrival(k).wait_recv(), NX)
+    square = parts[0] + parts[1] + parts[2] + parts[3]
+    square = jnp.sum(square, axis=1, keepdims=True)
+    key_rms = jnp.sqrt(square / (HEADS * HEAD_DIM) + EPSILON)
+    rms_out[...] = jnp.broadcast_to(key_rms, (T_DEV, HEAD_DIM))
+    normed[...] = (key_ref[...].astype(F32) / key_rms).astype(BF16)
+    own_slot_copy.wait()
+    own_meta_copy.wait()
+    z_start(3)
 
     def finish_small(k):
         small_arrival(0, k).wait_recv()
@@ -260,49 +333,41 @@
     keep_slots.start()
     meta_own().start()
     each(1, lambda k: meta_copy(k).start())
-
-    def build(zz, carry):
-        placing[zz] = expander(slots[zz], lax.rem(zz, 2))
+    each(0, lambda q: placing.__setitem__((q, 0), expander(slots[q], 0)), 4)
+    each(0, lambda q: placing.__setitem__((q, 1), expander(slots[q + 4], 1)), 4)
+
+    def expand(a, carry):
+        def pair(o):
+            q = lax.rem(z + o, 4)
+            pltpu.make_async_copy(held.at[a, q], held.at[a, q], z_recv.at[a, q]).wait()
+            rows = jnp.dot(placing[q, 0], held[a, q, 0], preferred_element_type=F32)
+            rows += jnp.dot(placing[q, 1], held[a, q, 1], preferred_element_type=F32)
+            sending[a, q] = rows.astype(BF16).reshape(ND, 2, PAIR, HEAD_DIM)
+            each(1, lambda k: d_copy(a, q, k).start())
+            pltpu.make_async_copy(
+                sending.at[a, q, d], landed.at[a, d, q], d_recv.at[a, d]
+            ).start()
+
+        each(0, pair, 4)
         return carry
 
-    lax.fori_loop(0, NZ, build, 0)
-
-    def expand(a, carry):
-        pltpu.make_async_copy(held.at[a, z], held.at[a, z], z_recv.at[a, z]).wait()
-        each(1, lambda k: z_arrival(a, k).wait_recv())
-
-        def pair(p, inner):
-            rows = jnp.dot(placing[2 * p], held[a, 2 * p], preferred_element_type=F32)
-            rows += jnp.dot(placing[2 * p + 1], held[a, 2 * p + 1], preferred_element_type=F32)
-            sending[a, p] = rows.astype(BF16).reshape(ND, 2, PAIR, HEAD_DIM)
-            return inner
-
-        lax.fori_loop(0, NZ // 2, pair, 0)
-        each(1, lambda k: d_copy(a, k).start())
-        d_own(a).start()
-        return carry
-
     lax.fori_loop(0, 4, expand, 0)
 
     def finish(a, carry):
-        d_own(a).wait()
+        pltpu.make_async_copy(landed.at[a, d], landed.at[a, d], d_recv.at[a, d]).wait()
         each(1, lambda k: d_arrival(a, k).wait_recv())
         put_out(a).start()
 
         def one(k):
             d_arrival(a, k).wait_send()
-            z_arrival(a, k).wait_send()
+            z_sent(a, k).wait_send()
 
         each(1, one)
         return carry
 
     lax.fori_loop(0, 4, finish, 0)
-
-    def close(a, carry):
-        put_out(a).wait()
-        return carry
-
-    lax.fori_loop(0, 4, close, 0)
+    each(0, lambda a: put_out(a).wait(), 4)
+    each(1, lambda k: x_arrival(k).wait_send(), NX)
     keep_slots.wait()
     meta_own().wait()
 
@@ -315,39 +380,48 @@
     each(1, finish_meta)
 
 
-def dispatch(slot_row, meta_row, v, g, q, k):
+def dispatch(ids, key, v, g, q):
     any_space = pl.BlockSpec(memory_space=pl.ANY)
+    near = pl.BlockSpec(memory_space=pltpu.VMEM)
     dma = pltpu.SemaphoreType.DMA
+    vmem = pltpu.VMEM
     return pl.pallas_call(
         dispatch_kernel,
         out_shape=(
             jax.ShapeDtypeStruct((4, ND, NZ // 2, 2, PAIR, HEAD_DIM), BF16),
             jax.ShapeDtypeStruct((ND, NZ, 1, 128), F32),
             jax.ShapeDtypeStruct((NZ, 1, 256), jnp.int32),
+            jax.ShapeDtypeStruct((T_DEV, HEAD_DIM), F32),
         ),
-        in_specs=[any_space] * 6,
-        out_specs=(any_space,) * 3,
+        in_specs=[near, near] + [any_space] * 3,
+        out_specs=(any_space,) * 3 + (near,),
         scratch_shapes=[
-            pltpu.VMEM((NZ, 1, 256), jnp.int32),
-            pltpu.VMEM((NZ, 1, 1024), F32),
-            pltpu.VMEM((4, NZ, T_DEV, HEAD_DIM), BF16),
-            pltpu.VMEM((NZ, ROWS, T_DEV), BF16),
-            pltpu.VMEM((4, NZ // 2, ND, 2, PAIR, HEAD_DIM), BF16),
-            pltpu.VMEM((4, ND, NZ // 2, 2, PAIR, HEAD_DIM), BF16),
+            vmem((1, 256), jnp.int32),
+            vmem((1, ND * 128), F32),
+            vmem((NZ, 1, 256), jnp.int32),
+            vmem((NZ, 1, ND * 128), F32),
+            vmem((NX, T_DEV, HEAD_DIM), F32),
+            vmem((T_DEV, NZ * HEAD_DIM), BF16),
+            vmem((4, NZ // 2, 2, T_DEV, HEAD_DIM), BF16),
+            vmem((NZ // 2, 2, ROWS, T_DEV), BF16),
+            vmem((4, NZ // 2, ND, 2, PAIR, HEAD_DIM), BF16),
+            vmem((4, ND, NZ // 2, 2, PAIR, HEAD_DIM), BF16),
             dma((4,)),
             dma((2, NZ)),
             dma((2, NZ)),
             dma((ND,)),
             dma((ND,)),
+            dma((NX,)),
+            dma((NX,)),
             dma((4, NZ)),
-            dma((4, NZ)),
+            dma((4, NZ // 2)),
             dma((4, ND)),
             dma((4, ND)),
             dma,
         ],
         compiler_params=pltpu.CompilerParams(collective_id=0, has_side_effects=True),
         name="dispatch",
-    )(slot_row, meta_row, v, g, q, k)
+    )(ids, key, v, g, q)
 
 
 def attention_kernel(
@@ -458,7 +532,8 @@
 def slot_tables():
     order = np.arange(SLOTS)
     rank = order % CAP
-    z = order // CAP % NZ
+    pair = order // CAP % NZ
+    z = pair // 2 + 4 * (pair % 2)
     d = order // (CAP * NZ)
     source = (d // 2) * 16 + z * 2 + d % 2
     arrival = d * NZ + z
@@ -523,11 +598,13 @@
 
 def combine_kernel(
     slots_ref,
+    key_ref,
+    rms_ref,
     dk_ref,
     o_ref,
     dq_ref,
     dv_ref,
-    dk_home,
+    key_home,
     o_home,
     dq_home,
     dv_home,
@@ -535,42 +612,54 @@
     placing,
     sending,
     landed,
+    parts,
+    key_done,
     out_sem,
     d_send,
     d_recv,
     z_send,
     z_recv,
+    x_send,
+    x_recv,
 ):
     y, z, core = place()
     d = y * 2 + core
+    x = lax.axis_index("head")
     sources = (dk_ref, o_ref, dq_ref, dv_ref)
-    homes = (dk_home, o_home, dq_home, dv_home)
-    greet(y, z, core, d)
-
-    def d_copy(a, k):
+    homes = (key_home, o_home, dq_home, dv_home)
+    barrier = greet(y, z, core, d, x)
+
+    across = lax.broadcasted_iota(jnp.int32, (T_DEV, T_DEV), 1)
+    down = lax.broadcasted_iota(jnp.int32, (T_DEV, T_DEV), 0)
+    eye = jnp.where(down == across, 1.0, 0.0).astype(BF16)
+
+    def build(zz):
+        there = expander(slots_ref[zz], zz // 4)
+        placing[zz] = contract_last(eye, there).astype(BF16)
+
+    def d_copy(a, q, k):
         to = lax.rem(d + k, ND)
         return pltpu.make_async_remote_copy(
-            src_ref=sources[a].at[to],
-            dst_ref=held.at[a, d],
+            src_ref=sources[a].at[to, q],
+            dst_ref=held.at[a, q, d],
             send_sem=d_send.at[a, to],
-            recv_sem=d_recv.at[a, d],
+            recv_sem=d_recv.at[a, q],
             device_id={"seq": along_d(to, z)},
             device_id_type=MESH,
         )
 
-    def d_arrival(a, k):
-        came = lax.rem(d + k, ND)
-        return pltpu.make_async_remote_copy(
-            src_ref=held.at[a, came],
-            dst_ref=held.at[a, came],
-            send_sem=d_send.at[a, came],
-            recv_sem=d_recv.at[a, came],
-            device_id={"seq": along_d(came, z)},
-            device_id_type=MESH,
-        )
-
-    def z_copy(a, k):
-        to = lax.rem(z + k, NZ)
+    def d_sent(a, k):
+        to = lax.rem(d + k, ND)
+        return pltpu.make_async_remote_copy(
+            src_ref=sources[0].at[to],
+            dst_ref=sources[0].at[to],
+            send_sem=d_send.at[a, to],
+            recv_sem=d_recv.at[a, 0],
+            device_id={"seq": along_d(to, z)},
+            device_id_type=MESH,
+        )
+
+    def z_copy(a, to):
         return pltpu.make_async_remote_copy(
             src_ref=sending.at[a, to],
             dst_ref=landed.at[a, :, head_columns(z)],
@@ -596,123 +685,154 @@
             sending.at[a, z], landed.at[a, :, head_columns(z)], z_recv.at[a, z]
         )
 
-    def each(first, body):
-        def step(k, carry):
-            body(k)
-            return carry
-
-        lax.fori_loop(first, 8, step, 0)
-
+    x_copy, x_arrival = x_copies(x, parts, x_send, x_recv)
+    pl.semaphore_wait(barrier, 17)
     for a in range(4):
-        each(1, lambda k, a=a: d_copy(a, k).start())
-        pltpu.make_async_copy(sources[a].at[d], held.at[a, d], d_recv.at[a, d]).start()
-
-    across = lax.broadcasted_iota(jnp.int32, (T_DEV, T_DEV), 1)
-    down = lax.broadcasted_iota(jnp.int32, (T_DEV, T_DEV), 0)
-    eye = jnp.where(down == across, 1.0, 0.0).astype(BF16)
-
-    def build(zz, carry):
-        there = expander(slots_ref[zz], lax.rem(zz, 2))
-        placing[zz] = contract_last(eye, there).astype(BF16)
+
+        def chunk_start(o, a=a):
+            q = lax.rem(z + o, 4)
+            each(1, lambda k: d_copy(a, q, k).start())
+            pltpu.make_async_copy(
+                sources[a].at[d, q], held.at[a, q, d], d_recv.at[a, q]
+            ).start()
+
+        each(0, chunk_start, 4)
+
+    each(0, build)
+
+    def gather(a, carry):
+        def chunk(o):
+            q = lax.rem(z + o, 4)
+            pltpu.make_async_copy(held.at[a, q], held.at[a, q], d_recv.at[a, q]).wait()
+            rows = held[a, q].reshape(ROWS, HEAD_DIM)
+            far = lax.rem(z + o + 4, NZ)
+            found = jnp.dot(placing[far], rows, preferred_element_type=F32)
+            sending[a, far] = found.astype(BF16)
+            z_copy(a, far).start()
+            close = lax.rem(z + o, NZ)
+            found = jnp.dot(placing[close], rows, preferred_element_type=F32)
+            sending[a, close] = found.astype(BF16)
+
+        chunk(0)
+        z_own(a).start()
+
+        def chunk_both(o):
+            chunk(o)
+            z_copy(a, lax.rem(z + o, NZ)).start()
+
+        each(1, chunk_both, 4)
         return carry
 
-    lax.fori_loop(0, NZ, build, 0)
-
-    for a in range(4):
-        pltpu.make_async_copy(held.at[a, d], held.at[a, d], d_recv.at[a, d]).wait()
-        each(1, lambda k, a=a: d_arrival(a, k).wait_recv())
-
-        def gather(k, a=a):
-            to = lax.rem(z + k, NZ)
-            rows = held[a, :, to // 2].reshape(ROWS, HEAD_DIM)
-            found = jnp.dot(placing[to], rows, preferred_element_type=F32)
-            sending[a, to] = found.astype(BF16)
-
-        def gather_send(k, a=a):
-            gather(k)
-            z_copy(a, k).start()
-
-        each(1, gather_send)
-        gather(0)
-        z_own(a).start()
+    lax.fori_loop(0, 4, gather, 0)
 
     def put_out(a):
-        return pltpu.make_async_copy(landed.at[a], homes[a], out_sem.at[a])
-
-    for a in range(4):
+        source = key_done if a == 0 else landed.at[a]
+        return pltpu.make_async_copy(source, homes[a], out_sem.at[a])
+
+    def home(a):
         z_own(a).wait()
-        each(1, lambda k, a=a: z_arrival(a, k).wait_recv())
-        put_out(a).start()
+        each(1, lambda k: z_arrival(a, k).wait_recv())
+
+    home(0)
+    key_float = key_ref[...].astype(F32)
+    rms = rms_ref[:, 0:1]
+    normed_float = key_float / rms
+    parts[x] = lanes_summed(normed_float * landed[0].astype(F32))
+    each(1, lambda k: x_copy(k).start(), NX)
+    home(1)
+    put_out(1).start()
+    home(2)
+    put_out(2).start()
+    each(1, lambda k: x_arrival(k).wait_recv(), NX)
+    inner = parts[0] + parts[1] + parts[2] + parts[3]
+    inner = jnp.sum(inner, axis=1, keepdims=True) / (HEADS * HEAD_DIM)
+    key_grad = (landed[0].astype(F32) - normed_float * inner) / rms
+    key_done[...] = key_grad.astype(BF16)
+    put_out(0).start()
+    home(3)
+    put_out(3).start()
+    each(1, lambda k: x_arrival(k).wait_send(), NX)
 
     for a in range(4):
 
         def one(k, a=a):
             z_arrival(a, k).wait_send()
-            d_arrival(a, k).wait_send()
+            d_sent(a, k).wait_send()
 
         each(1, one)
         put_out(a).wait()
 
 
-def combine(slots, dk, o, dq, dv):
+def combine(slots, key, rms, dk, o, dq, dv):
     any_space = pl.BlockSpec(memory_space=pl.ANY)
+    near = pl.BlockSpec(memory_space=pltpu.VMEM)
     dma = pltpu.SemaphoreType.DMA
+    vmem = pltpu.VMEM
     home = jax.ShapeDtypeStruct((T_DEV, NZ * HEAD_DIM), BF16)
     return pl.pallas_call(
         combine_kernel,
         out_shape=(home,) * 4,
-        in_specs=[pl.BlockSpec(memory_space=pltpu.VMEM)] + [any_space] * 4,
+        in_specs=[near] * 3 + [any_space] * 4,
         out_specs=(any_space,) * 4,
         scratch_shapes=[
-            pltpu.VMEM((4, ND, NZ // 2, 2, PAIR, HEAD_DIM), BF16),
-            pltpu.VMEM((NZ, T_DEV, ROWS), BF16),
-            pltpu.VMEM((4, NZ, T_DEV, HEAD_DIM), BF16),
-            pltpu.VMEM((4, T_DEV, NZ * HEAD_DIM), BF16),
+            vmem((4, NZ // 2, ND, 2, PAIR, HEAD_DIM), BF16),
+            vmem((NZ, T_DEV, ROWS), BF16),
+            vmem((4, NZ, T_DEV, HEAD_DIM), BF16),
+            vmem((4, T_DEV, NZ * HEAD_DIM), BF16),
+            vmem((NX, T_DEV, HEAD_DIM), F32),
+            vmem((T_DEV, NZ * HEAD_DIM), BF16),
             dma((4,)),
             dma((4, ND)),
-            dma((4, ND)),
+            dma((4, NZ // 2)),
             dma((4, NZ)),
             dma((4, NZ)),
+            dma((NX,)),
+            dma((NX,)),
         ],
         compiler_params=pltpu.CompilerParams(collective_id=1, has_side_effects=True),
         name="combine",
-    )(slots, dk, o, dq, dv)
+    )(slots, key, rms, dk, o, dq, dv)
+
+
+def hand_over_kernel(*refs):
+    ins, outs, held, in_sem, out_sem = refs[0:4], refs[4:8], refs[8], refs[9], refs[10]
+    arrive = [pltpu.make_async_copy(ins[a], held.at[a], in_sem.at[a]) for a in range(4)]
+    leave = [pltpu.make_async_copy(held.at[a], outs[a], out_sem.at[a]) for a in range(4)]
+    for a in range(4):
+        arrive[a].start()
+    for a in range(4):
+        arrive[a].wait()
+        leave[a].start()
+    for a in range(4):
+        leave[a].wait()
+
+
+def hand_over(*arrays):
+    any_space = pl.BlockSpec(memory_space=pl.ANY)
+    dma = pltpu.SemaphoreType.DMA
+    return pl.pallas_call(
+        hand_over_kernel,
+        out_shape=tuple(jax.ShapeDtypeStruct(a.shape, a.dtype) for a in arrays),
+        in_specs=[any_space] * 4,
+        out_specs=(any_space,) * 4,
+        scratch_shapes=[pltpu.VMEM((4,) + arrays[0].shape, BF16), dma((4,)), dma((4,))],
+        name="hand_over",
+    )(*arrays)
 
 
 def per_device(queries, key_vectors, values, cotangent, cluster, block_pattern):
     me = lax.axis_index("seq")
     d = (me // (2 * NZ)) * 2 + me % 2
-    key_float = key_vectors.astype(F32)
-    square_sum = lax.psum(jnp.sum(key_float * key_float, axis=1), "head")
-    key_rms = jnp.sqrt(square_sum / (HEADS * HEAD_DIM) + EPSILON)[:, None]
-    normed_float = key_float / key_rms
-    normed = normed_float.astype(BF16)
-    ids = cluster[:, 0]
-    token = jnp.arange(T_DEV, dtype=jnp.int32)
-    earlier = (ids[:, None] == ids[None, :]) & (token[:, None] < token[None, :])
-    rank = jnp.sum(earlier.astype(jnp.int32), axis=0)
-    slot = ids * PAIR + rank
-    slot_row = jnp.pad(slot, (0, 256 - T_DEV), constant_values=-1).reshape(1, 256)
-    meta_slot = (ids // 2) * 128 + (ids % 2) * CAP + rank
-    spots = jnp.arange(ND * 128, dtype=jnp.int32)
-    hit = meta_slot[:, None] == spots[None, :]
-    meta_row = jnp.sum(jnp.where(hit, (token + 1).astype(F32)[:, None], 0.0), axis=0)
-    arrived, meta, slots = dispatch(
-        slot_row, meta_row.reshape(1, ND * 128), values, cotangent, queries, normed
-    )
+    ids = cluster.reshape(1, T_DEV)
+    arrived, meta, slots, rms = dispatch(ids, key_vectors, values, cotangent, queries)
     pattern = lax.dynamic_slice_in_dim(block_pattern, 2 * d, 2, 0)
     blocks = pattern.shape[1]
     pattern = jnp.where(pattern == 1, 0.0, -BIG)
     pattern = jnp.pad(pattern, ((0, 0), (0, 0), (0, 1)), constant_values=-BIG)
     pattern = jnp.pad(pattern, ((0, 0), (0, 128 - blocks), (0, 127 - blocks))).astype(BF16)
     o, dq, dk, dv = attention(meta.reshape(64, 128), pattern, arrived)
-    grad_rows, attended, query_grad, value_grad = combine(slots, dk, o, dq, dv)
-    grad_float = grad_rows.astype(F32)
-    inner = lax.psum(jnp.sum(normed_float * grad_float, axis=1), "head")
-    key_grad = (
-        (grad_float - normed_float * (inner / (HEADS * HEAD_DIM))[:, None]) / key_rms
-    ).astype(BF16)
-    return (attended, query_grad, key_grad, value_grad)
+    key_grad, attended, query_grad, value_grad = combine(slots, key_vectors, rms, dk, o, dq, dv)
+    return hand_over(attended, query_grad, key_grad, value_grad)
 
 
 def solution(mesh):

time: 170 us -> 135 us (0.79)
  blocking collectives: 15.3 us -> 0 us
  other arithmetic: 10.9 us -> 1.56 us
  local copies, waits for them, and re-layouts: 4.85 us -> 0 us
  Pallas kernels: 137 us -> 133 us
    psum x2 -> x0, blocking collectives: 15.3 us -> none  [the longest x1 9.29 us: per_device(): square_sum = lax.psum(jnp.sum(key_float * key_float, axis=1), 'head')]
    unnamed x7 -> x0, local copies, waits for them, and re-layouts: 4.29 us -> none
    reduce_sum x4 -> x0, other arithmetic: 4.1 us -> none  [the longest x1 1.33 us: per_device(): inner = lax.psum(jnp.sum(normed_float * grad_float, axis=1), 'head')]
    convert_element_type x3 -> x0, other arithmetic: 3.9 us -> none  [the longest x1 2 us: per_device(): key_grad = ((grad_float - normed_float * (inner / (HEADS * HEAD_DIM))[:,...]
    pallas_call x1 -> x2, Pallas kernels: 54.9 us -> 52.5 us  [the longest x1 50.3 us: combine(): pl.pallas_call(combine_kernel, out_shape=(home,) * 4, in_specs=[near] * 3...]
    pallas_call x1, Pallas kernels: 60.7 us -> 58.5 us  [dispatch(): pl.pallas_call(dispatch_kernel, out_shape=(jax.ShapeDtypeStruct((4, ND, N...]
where the time goes in v3:
time: 135 us
  Pallas kernels  133 us (99%)
  other arithmetic  1.56 us (1%)
    pallas_call x1, Pallas kernels, dispatch(): pl.pallas_call(dispatch_kernel, out_shape=(jax.ShapeDtypeStruct((4, ND, N...  58.5 us
    pallas_call x1, Pallas kernels, combine(): pl.pallas_call(combine_kernel, out_shape=(home,) * 4, in_specs=[near] * 3...  50.3 us
    pallas_call x1, Pallas kernels, attention(): pl.pallas_call(functools.partial(attention_kernel, HEAD_DIM ** (-0.5)), o...  21.7 us

profile of v3, /device:TPU:1, one launch (start us, length us, event | category | flops | bytes accessed | tf_op | source)
XLA Modules:
  0.0 135.0 jit_solution(17981600502050362226)
XLA Ops:
  0.7 0.9 select_convert_fusion
  1.6 0.6 fusion.2.pattern_ref
  2.2 58.5 %dispatch.1 = (bf16[4,8,4,2,48,128]{5,4,3,2,1,0:T(8,128)(2,1)}, f32[8,8,1,128]{3,2,1,0:T(1,128)}, s32[8,1,256]{2,1,0:T(1,128)}, f32[192,128]{1,0:T(8,128)}) custom-call(s32[1,192]{1,0:T(1,128)} %bitcast.3, bf16[192,1024]{1,0:T(8,128)(2,1)} %key_ref.3, bf16[192,1024]{1,0:T(8,128)(2,1)} %v_ref.1, bf16[192,1024]{1,0:T(8,128)(2,1)} %g_ref.1, bf16[192,1024]{1,0:T(8,128)(2,1)} %q_ref.1), custom_call_target="tpu_custom_call" | custom-call | tf_op jit(solution)/shard_map/dispatch/pallas_call | solution.py:388
  60.7 21.7 %attention.1 = (bf16[8,4,2,48,128]{4,3,2,1,0:T(8,128)(2,1)}, bf16[8,4,2,48,128]{4,3,2,1,0:T(8,128)(2,1)}, bf16[8,4,2,48,128]{4,3,2,1,0:T(8,128)(2,1)}, bf16[8,4,2,48,128]{4,3,2,1,0:T(8,128)(2,1)}) custom-call(f32[64,128]{1,0:T(8,128)} %bitcast.2, bf16[1536,64]{1,0:T(8,128)(2,1)} %constant.53.clone.rep_ref, bf16[2,1536,128]{2,1,0:T(8,128)(2,1)} %constant.54.clone.pick_ref, ...), custom_call_target="tpu_custom_call" | custom-call | tf_op jit(solution)/shard_map/attention/pallas_call | solution.py:566
  82.5 50.3 %combine.1 = (bf16[192,1024]{1,0:T(8,128)(2,1)}, bf16[192,1024]{1,0:T(8,128)(2,1)}, bf16[192,1024]{1,0:T(8,128)(2,1)}, bf16[192,1024]{1,0:T(8,128)(2,1)}) custom-call(s32[8,1,256]{2,1,0:T(1,128)} %get-tuple-element.16.slots_ref, bf16[192,1024]{1,0:T(8,128)(2,1)} %key_ref.3, f32[192,128]{1,0:T(8,128)} %get-tuple-element.17.rms_ref, ...), custom_call_target="tpu_custom_call" | custom-call | tf_op jit(solution)/shard_map/combine/pallas_call | solution.py:772
  132.8 2.2 %hand_over.1 = (bf16[192,1024]{1,0:T(8,128)(2,1)}, bf16[192,1024]{1,0:T(8,128)(2,1)}, bf16[192,1024]{1,0:T(8,128)(2,1)}, bf16[192,1024]{1,0:T(8,128)(2,1)}) custom-call(bf16[192,1024]{1,0:T(8,128)(2,1)} %get-tuple-element.24.refs_0_, bf16[192,1024]{1,0:T(8,128)(2,1)} %get-tuple-element.25.refs_1_, bf16[192,1024]{1,0:T(8,128)(2,1)} %get-tuple-element.26.refs_2_, ...), custom_call_target="tpu_custom_call" | custom-call | tf_op jit(solution)/shard_map/hand_over/pallas_call | solution.py:813
